TPU v7x, 256 devices: a whole 4x4x8 slice. The times are simulated.
256 devices in a mesh: tm: 8 (over y, core), space: 32 (over z, x).
Axes of the slice: x: 4, y: 4, z: 8, core: 2. Of those that a mesh axis runs over, the one named last changes fastest.
Arguments:
- background: bfloat16 [262144, 64], P('space'), may hold values from -4 to 4
- probe: bfloat16 [64, 32], replicated, may hold values from -0.75 to 0.75
- member_scale: float32 [64], replicated, may hold values from 0.5 to 2
- decay: float32 [24, 32], P('tm'), may hold values from 0.36 to 1
- inflation: float32 [24], P('tm'), may hold values from 0.05 to 0.5
- obs_owner: int32 [24, 65536, 1], P('tm', 'space'), may hold values from 0 to 31; in each aligned block of 2048 rows (0 to 2047, 2048 to 4095, ..., all dimensions but the last counted through in order) at most 128 rows name the same one
- obs_offset: int32 [24, 65536], P('tm', 'space'), may hold values from 0 to 8191
- obs_value: float32 [24, 65536], P('tm', 'space'), may hold values from -360 to 360
- obs_weight: float32 [24, 65536], P('tm', 'space'), may hold values from 0.0002 to 0.002
Outputs:
- smooth_mean: float32 [24, 262144], P('tm', 'space')
- smooth_spread: float32 [24, 262144], P('tm', 'space')
Inputs may be any that keep to these rules, and one draw needn't show every extreme that they name: `obs_owner`: of the 2048 observations that one reader holds for one day, at most 128 name the same owner, and 128 is reached.
All inputs are finite; a program needn't handle non-finite values.
Results may differ from a plain program's by a relative error of at most 0.0029.
Values sent between devices are 32-bit elements; how exact they have to be, the bound alone decides.
No kernel may reach another device: no remote copies, remote signals or barrier semaphores. Data moves between devices by JAX's collectives and lax.ppermute only.
A program may use at most 64 MiB of HBM per device.

v0:
```python
import jax
import jax.numpy as jnp
from jax import lax
from jax.sharding import PartitionSpec as P

HIGHEST = lax.Precision.HIGHEST


def copy_for_each(shard, axis):
    peers = lax.axis_size(axis)
    return lax.all_to_all(
        jnp.broadcast_to(shard[None], (peers, *shard.shape)), axis, 0, 0, tiled=True
    )


def of_everyone(shard, axis):
    return copy_for_each(shard, axis).sum(axis=0)


def together(arrays, axis):
    flat, at, outs = (jnp.concatenate([a.reshape(-1) for a in arrays]), 0, [])
    so_far = of_everyone(flat, axis)
    for a in arrays:
        outs.append(so_far[at : at + a.size].reshape(a.shape))
        at += a.size
    return tuple(outs)


def collected_together(shard, axis):
    leaves = jax.tree.leaves(shard)
    order = sorted(range(len(leaves)), key=lambda k: -leaves[k].size)
    width = (1, *leaves[order[0]].shape)[-1]
    lines = [
        jnp.pad(leaves[k].reshape(-1), (0, -leaves[k].size % width)).reshape(-1, width)
        for k in order
    ]
    both, at, found = (copy_for_each(jnp.concatenate(lines), axis), 0, {})
    for k, line in zip(order, lines):
        section = both[:, at : at + len(line)].reshape(len(both), -1)
        found[k] = section[:, : leaves[k].size].reshape(-1, *leaves[k].shape)
        at += len(line)
    numbers = iter(range(len(leaves)))
    return jax.tree.map(lambda _: found[next(numbers)], shard)


def joined_by_halves(pieces, combine):
    while len(jax.tree.leaves(pieces)[0]) > 1:
        pieces = jax.vmap(combine)(
            *(jax.tree.map(lambda part: part[side::2], pieces) for side in (0, 1))
        )
    return jax.tree.map(lambda part: part[0], pieces)


def prefix(shard, axis, combine, identity):
    peers, position = (lax.axis_size(axis), lax.axis_index(axis))
    passed = jnp.arange(peers) < position

    def kept(part, zero, own):
        part = jnp.where(
            passed.reshape(-1, *(1 for _ in own.shape)), part, jnp.asarray(zero, own.dtype)
        )
        return part

    pieces = collected_together(shard, axis)
    return joined_by_halves(jax.tree.map(kept, pieces, identity, shard), combine)


def passed_along(value, axis, steps):
    count = lax.axis_size(axis)
    initial, last = (max(0, -steps), min(count, count - steps))
    return lax.ppermute(value, axis, [(source, source + steps) for source in range(initial, last)])


def collected_alike(shard, axis):
    leaves, found = (jax.tree.leaves(shard), {})
    for initial, a in enumerate(leaves):
        if initial not in found:
            alike = [k for k, b in enumerate(leaves) if b.dtype == a.dtype]
            got = (
                collected_together([leaves[k] for k in alike], axis)
                if len(alike) > 1
                else [copy_for_each(a, axis)]
            )
            for k, b in zip(alike, got):
                found[k] = b
    numbers = iter(range(len(leaves)))
    return jax.tree.map(lambda _: found[next(numbers)], shard)


def prefix_2(shard, axis, combine, identity):
    peers, position = (lax.axis_size(axis), lax.axis_index(axis))
    passed = jnp.arange(peers) > position

    def kept(part, zero, own):
        part = jnp.where(
            passed.reshape(-1, *(1 for _ in own.shape)), part, jnp.asarray(zero, own.dtype)
        )
        return part[::-1]

    pieces = collected_alike(shard, axis)
    return joined_by_halves(jax.tree.map(kept, pieces, identity, shard), combine)


def matmul_high(left_mat, right_mat):
    return jnp.matmul(left_mat, right_mat, precision=HIGHEST)


def matvec_high(matrix, vector):
    return matmul_high(matrix, vector[..., None])[..., 0]


def flip_last(matrix):
    return jnp.swapaxes(matrix, -1, -2)


def symmetric(matrix):
    return 0.5 * (matrix + flip_last(matrix))


def spd_solve(matrix, right_side):
    lower_chol = jnp.linalg.cholesky(matrix)
    middle = lax.linalg.triangular_solve(lower_chol, right_side, left_side=True, lower=True)
    return lax.linalg.triangular_solve(
        lower_chol, middle, left_side=True, lower=True, transpose_a=True
    )


def spd_inverse(matrix):
    identity_mat = jnp.broadcast_to(jnp.eye(matrix.shape[-1], dtype=jnp.float32), matrix.shape)
    return spd_solve(matrix, identity_mat)


def filter_combine(left_elem, right_elem):
    trans_a, mean_a, cov_a, vec_a, prec_a = left_elem
    trans_b, mean_b, cov_b, vec_b, prec_b = right_elem
    width = cov_a.shape[-1]
    coupled = jnp.eye(width, dtype=jnp.float32) + matmul_high(cov_a, prec_b)
    normal_mat = matmul_high(flip_last(coupled), coupled)
    coupled_inv = spd_solve(normal_mat, flip_last(coupled))
    left_gain = matmul_high(trans_b, coupled_inv)
    transition = matmul_high(left_gain, trans_a)
    mean_out = matvec_high(left_gain, mean_a + matvec_high(cov_a, vec_b)) + mean_b
    cov_out = symmetric(matmul_high(matmul_high(left_gain, cov_a), flip_last(trans_b)) + cov_b)
    back_gain = matmul_high(flip_last(trans_a), flip_last(coupled_inv))
    vec_out = matvec_high(back_gain, vec_b - matvec_high(prec_b, mean_a)) + vec_a
    prec_out = symmetric(matmul_high(matmul_high(back_gain, prec_b), trans_a) + prec_a)
    return (transition, mean_out, cov_out, vec_out, prec_out)


def smooth_combine(left_elem, right_elem):
    gain_a, mean_a, cov_a = left_elem
    gain_b, mean_b, cov_b = right_elem
    gain_out = matmul_high(gain_a, gain_b)
    mean_out = matvec_high(gain_a, mean_b) + mean_a
    cov_out = symmetric(matmul_high(matmul_high(gain_a, cov_b), flip_last(gain_a)) + cov_a)
    return (gain_out, mean_out, cov_out)


def make_reader(rows_source, received):
    values = received[0]
    weights = received[1]
    offsets = received[2].astype(jnp.int32)
    basis_rows = rows_source[offsets]
    weighted = basis_rows * weights[..., None]
    core_part = jnp.einsum("sdcr,sdcq->drq", weighted, basis_rows, precision=HIGHEST)
    vector_part = jnp.einsum("sdcr,sdc->dr", weighted, values, precision=HIGHEST)
    return (core_part, vector_part)


def subspace_setup(member_gram, probe_wide, field_basis, member_scale):
    mode_count = probe_wide.shape[1]
    core_gram = matmul_high(matmul_high(probe_wide.T, member_gram), probe_wide)
    lower_chol = jnp.linalg.cholesky(core_gram)
    lower_inv = lax.linalg.triangular_solve(
        lower_chol, jnp.eye(mode_count, dtype=jnp.float32), left_side=True, lower=True
    )
    basis = matmul_high(field_basis, lower_inv.T)
    projected = matmul_high(lower_inv, matmul_high(probe_wide.T, member_gram))
    prior_cov = matmul_high(projected * (member_scale * member_scale)[None, :], projected.T)
    return (lower_inv, basis, prior_cov)


def body(
    background, probe, member_scale, decay, inflation, obs_owner, obs_offset, obs_value, obs_weight
):
    mode_count = probe.shape[1]
    days_dev = decay.shape[0]
    obs_dev = obs_offset.shape[1]
    space_count = lax.axis_size("space")
    time_count = lax.axis_size("tm")
    time_index = lax.axis_index("tm")
    bucket_cap = 2 * obs_dev // space_count
    identity_mat = jnp.eye(mode_count, dtype=jnp.float32)
    zero_mat = jnp.zeros((mode_count, mode_count), jnp.float32)
    zero_vec = jnp.zeros((mode_count,), jnp.float32)
    scaled_probe = (probe.astype(jnp.float32) * member_scale[:, None]).astype(jnp.bfloat16)
    probe_wide = scaled_probe.astype(jnp.float32)
    field_basis = jnp.dot(background, scaled_probe, preferred_element_type=jnp.float32)
    local_gram = jnp.dot(background.T, background, preferred_element_type=jnp.float32)
    owners = obs_owner[:, :, 0]
    owner_hits = (
        owners[:, :, None] == jnp.arange(space_count, dtype=jnp.int32)[None, None, :]
    ).astype(jnp.int32)
    earlier_hits = jnp.cumsum(owner_hits, axis=1) - owner_hits
    slot_index = jnp.sum(earlier_hits * owner_hits, axis=2)
    day_index = jnp.broadcast_to(jnp.arange(days_dev, dtype=jnp.int32)[:, None], owners.shape)
    packed = jnp.stack([obs_value, obs_weight, obs_offset.astype(jnp.float32)], axis=0)
    buckets = (
        jnp.zeros((3, space_count, days_dev, bucket_cap), jnp.float32)
        .at[:, owners, day_index, slot_index]
        .set(packed)
    )
    core_field, vector_field = make_reader(
        field_basis, lax.all_to_all(buckets, "space", split_axis=1, concat_axis=1, tiled=True)
    )
    member_gram, core_field, vector_field = together(
        (local_gram, core_field, vector_field), "space"
    )
    lower_inv, basis, prior_cov = subspace_setup(member_gram, probe_wide, field_basis, member_scale)
    precision_core = matmul_high(matmul_high(lower_inv, core_field), lower_inv.T)
    info_vector = matmul_high(vector_field, lower_inv.T)
    noise_cov = inflation[:, None, None] * prior_cov
    noise_inv = spd_inverse(noise_cov)
    elem_cov = symmetric(spd_inverse(noise_inv + precision_core))
    elem_trans = matmul_high(elem_cov, noise_inv) * decay[:, None, :]
    elem_mean = matvec_high(elem_cov, info_vector)
    corrected = precision_core - matmul_high(matmul_high(precision_core, elem_cov), precision_core)
    elem_prec = decay[:, :, None] * corrected * decay[:, None, :]
    elem_vec = decay * (info_vector - matvec_high(precision_core, elem_mean))
    elements = (elem_trans, elem_mean, elem_cov, elem_vec, elem_prec)
    prior_elem = (zero_mat, zero_vec, prior_cov, zero_vec, zero_mat)
    first_elem = tuple((member[0] for member in elements))
    merged = filter_combine(prior_elem, first_elem)
    is_opening_day = time_index == 0
    elements = tuple(
        (
            member.at[0].set(jnp.where(is_opening_day, joined, member[0]))
            for member, joined in zip(elements, merged)
        )
    )
    local_prefix = lax.associative_scan(filter_combine, elements)
    total_trans, total_mean, total_cov, total_vec, total_prec = tuple(
        (member[-1] for member in local_prefix)
    )
    filter_identity = (identity_mat, zero_vec, zero_mat, zero_vec, zero_mat)
    from_left = prefix(
        (total_trans, total_mean, total_cov, total_vec, total_prec),
        "tm",
        filter_combine,
        filter_identity,
    )
    filtered = filter_combine(from_left, local_prefix)
    filt_mean = filtered[1]
    filtered_covariance = filtered[2]
    next_decay, next_infl = passed_along((decay[0:1], inflation[0:1]), "tm", -1)
    decay_next = jnp.concatenate([decay[1:], next_decay], axis=0)
    infl_next = jnp.concatenate([inflation[1:], next_infl], axis=0)
    day_pos = jnp.arange(days_dev, dtype=jnp.int32)
    is_last = jnp.logical_and(time_index == time_count - 1, day_pos == days_dev - 1)
    infl_next = jnp.where(is_last, 1.0, infl_next)
    predicted = (
        decay_next[:, :, None] * filtered_covariance * decay_next[:, None, :]
        + infl_next[:, None, None] * prior_cov
    )
    rescaled_covariance = decay_next[:, :, None] * filtered_covariance
    gain_days = flip_last(spd_solve(predicted, rescaled_covariance))
    shifted_mean = filt_mean - matvec_high(gain_days, decay_next * filt_mean)
    resid_cov = symmetric(filtered_covariance - matmul_high(gain_days, rescaled_covariance))
    gain_days = jnp.where(is_last[:, None, None], 0.0, gain_days)
    shifted_mean = jnp.where(is_last[:, None], filt_mean, shifted_mean)
    resid_cov = jnp.where(is_last[:, None, None], filtered_covariance, resid_cov)

    def reverse_local(after_part, before_part):
        return smooth_combine(before_part, after_part)

    local_suffix = lax.associative_scan(
        reverse_local, (gain_days, shifted_mean, resid_cov), reverse=True
    )
    head_gain, head_mean, head_cov = tuple((member[0] for member in local_suffix))
    smooth_identity = (identity_mat, zero_vec, zero_mat)
    from_right = prefix_2((head_gain, head_mean, head_cov), "tm", reverse_local, smooth_identity)
    smoothed = smooth_combine(local_suffix, from_right)
    sm_mean = smoothed[1]
    sm_cov = smoothed[2]
    smooth_mean = matmul_high(sm_mean, basis.T)

    def spread_day(cov_day):
        return jnp.sum(matmul_high(basis, cov_day) * basis, axis=1)

    smooth_spread = lax.map(spread_day, sm_cov)
    return (smooth_mean, smooth_spread)


def solution(mesh):
    return jax.shard_map(
        body,
        mesh=mesh,
        in_specs=(
            P("space", None),
            P(),
            P(),
            P("tm", None),
            P("tm"),
            P("tm", "space", None),
            P("tm", "space"),
            P("tm", "space"),
            P("tm", "space"),
        ),
        out_specs=(P("tm", "space"), P("tm", "space")),
        check_vma=False,
    )
```

profile of v0, /device:TPU:1, one launch (start us, length us, event | category | flops | bytes accessed | tf_op | source)
XLA Modules:
  0.0 373.8 jit_solution(10577171297475330098)
XLA Ops:
  2.3 27.2 %reduce-window.6 = s32[3,32,16,128]{3,2,1,0:T(8,128)S(1)} reduce-window(s32[3,32,16,128]{3,2,1,0:T(8,128)S(1)} %fusion.46, s32[]{:T(128)} %constant.343.clone.1), window={size=1x1x1x128 pad=0_0x0_0x0_0x127_0}, to_apply=%region_0.0 | reduce-window | flops 24969216 | bytes 1572868 | tf_op jit(solution)/shard_map/reduce-window
  34.4 18.9 %scatter_custom_fusion = f32[3,12288]{0,1:T(8,128)} fusion(s32[6144]{0:T(1024)S(1)} %reshape.769, f32[6144,3]{1,0:T(8,128)} %bitcast.883, f32[]{:T(128)} %constant.342.clone.1), kind=kCustom, calls=%fused_computation.8 | custom fusion | bytes 147968
  53.3 5.5 %copy.484 = f32[3,3,32,128]{3,1,0,2:T(4,128)} copy(f32[3,3,32,128]{0,3,2,1:T(8,128)} %bitcast.879) | data formatting | bytes 294912
  58.8 11.9 %all-to-all-start = ((f32[3,32,3,128]{3,2,0,1:T(4,128)}), f32[3,32,3,128]{3,2,0,1:T(4,128)S(1)}, u32[]{:S(2)}, u32[]{:S(2)}) async-start(f32[3,32,3,128]{3,2,0,1:T(4,128)} %bitcast.14), calls=%async_computation | async-start | bytes 393216 | tf_op jit(solution)/shard_map/all_to_all | solution.py:214
  74.2 6.4 %all-to-all-done = f32[3,32,3,128]{3,2,0,1:T(4,128)S(1)} async-done(((f32[3,32,3,128]{3,2,0,1:T(4,128)}), f32[3,32,3,128]{3,2,0,1:T(4,128)S(1)}, u32[]{:S(2)}, u32[]{:S(2)}) %all-to-all-start) | async-done | bytes 147488 | tf_op jit(solution)/shard_map/all_to_all | solution.py:214
  80.7 43.2 %gather_fusion = f32[12288,32]{1,0:T(8,128)} fusion(f32[8192,32]{1,0:T(8,128)} %copy.487, s32[12288]{0:T(1024)S(1)} %broadcast_clamp_fusion), kind=kCustom, calls=%fused_computation | custom fusion | bytes 3194880 | tf_op jit(solution)/shard_map/gather | solution.py:163
  123.9 5.5 %copy.489 = f32[32,3,128,32]{2,3,0,1:T(8,128)} copy(f32[32,3,128,32]{3,2,1,0:T(8,128)} %bitcast.880) | data formatting | bytes 3145728 | tf_op jit(solution)/shard_map/gather | solution.py:163
  136.3 4.6 %all-to-all-start.1 = ((f32[32,1,7264]{2,1,0:T(1,128)}), f32[32,1,7264]{2,1,0:T(1,128)S(1)}, u32[]{:S(2)}, u32[]{:S(2)}) async-start(f32[32,1,7264]{2,1,0:T(1,128)} %broadcast_in_dim.238), calls=%async_computation.1 | async-start | bytes 1867776 | tf_op jit(solution)/shard_map/all_to_all | solution.py:11
  151.9 12.1 %all-to-all-done.1 = f32[32,1,7264]{2,1,0:T(1,128)S(1)} async-done(((f32[32,1,7264]{2,1,0:T(1,128)}), f32[32,1,7264]{2,1,0:T(1,128)S(1)}, u32[]{:S(2)}, u32[]{:S(2)}) %all-to-all-start.1) | async-done | bytes 929824 | tf_op jit(solution)/shard_map/all_to_all | solution.py:11
  173.1 8.8 %custom-call.66 = f32[3,32,32]{2,1,0:T(8,128)S(1)} custom-call(f32[3,32,32]{2,1,0:T(8,128)S(1)} %fusion.103), custom_call_target="Cholesky" | custom-call | tf_op jit(solution)/shard_map/jit(cholesky)/cholesky | solution.py:121
  182.1 7.4 %custom-call.68 = f32[3,1,32,32]{2,3,1,0:T(8,128)S(1)} custom-call(f32[3,1,32,32]{3,2,1,0:T(8,128)S(1)} %select_bitcast_fusion.4), custom_call_target="InvertDiagBlocksLowerTriangular" | custom-call | tf_op jit(solution)/shard_map/triangular_solve/custom-call.7 | solution.py:123
  190.2 8.8 %custom-call.69 = f32[3,32,32]{2,1,0:T(8,128)S(1)} custom-call(f32[3,32,32]{2,1,0:T(8,128)S(1)} %fusion.98), custom_call_target="Cholesky" | custom-call | tf_op jit(solution)/shard_map/jit(cholesky)/cholesky | solution.py:121
  199.2 7.4 %custom-call.71 = f32[3,1,32,32]{2,3,1,0:T(8,128)S(1)} custom-call(f32[3,1,32,32]{3,2,1,0:T(8,128)S(1)} %select_bitcast_fusion.3), custom_call_target="InvertDiagBlocksLowerTriangular" | custom-call | tf_op jit(solution)/shard_map/triangular_solve/custom-call.7 | solution.py:123
  239.4 7.9 %all-to-all-start.2 = ((f32[8,98,32]{1,2,0:T(8,128)}), f32[8,98,32]{1,2,0:T(8,128)S(1)}, u32[]{:S(2)}, u32[]{:S(2)}) async-start(f32[8,98,32]{1,2,0:T(8,128)} %broadcast_in_dim.250), calls=%async_computation.2 | async-start | bytes 262144 | tf_op jit(solution)/shard_map/all_to_all | solution.py:11
  254.5 11.7 %custom-call.45 = f32[4,32,32]{2,1,0:T(8,128)S(1)} custom-call(f32[4,32,32]{2,1,0:T(8,128)S(1)} %copy.536), custom_call_target="Cholesky" | custom-call | tf_op jit(solution)/shard_map/vmap(jit(cholesky))/cholesky | solution.py:121
  267.9 9.8 %custom-call.46 = f32[4,1,32,32]{2,3,1,0:T(8,128)S(1)} custom-call(f32[4,1,32,32]{3,2,1,0:T(8,128)S(1)} %select_bitcast_fusion), custom_call_target="InvertDiagBlocksLowerTriangular" | custom-call | tf_op jit(solution)/shard_map/vmap()/triangular_solve | solution.py:123
  280.6 5.9 %custom-call.47 = f32[2,32,32]{2,1,0:T(8,128)S(1)} custom-call(f32[2,32,32]{2,1,0:T(8,128)S(1)} %fusion.113), custom_call_target="Cholesky" | custom-call | tf_op jit(solution)/shard_map/vmap(jit(cholesky))/cholesky | solution.py:121
  286.7 4.9 %custom-call.48 = f32[2,1,32,32]{2,3,1,0:T(8,128)S(1)} custom-call(f32[2,1,32,32]{3,2,1,0:T(8,128)S(1)} %select_bitcast_fusion.6), custom_call_target="InvertDiagBlocksLowerTriangular" | custom-call | tf_op jit(solution)/shard_map/vmap()/triangular_solve | solution.py:123
  304.0 8.8 %custom-call.82 = f32[3,32,32]{2,1,0:T(8,128)S(1)} custom-call(f32[3,32,32]{2,1,0:T(8,128)S(1)} %fusion.90), custom_call_target="Cholesky" | custom-call | tf_op jit(solution)/shard_map/jit(cholesky)/cholesky | solution.py:121
  313.0 7.4 %custom-call.84 = f32[3,1,32,32]{2,3,1,0:T(8,128)S(1)} custom-call(f32[3,1,32,32]{3,2,1,0:T(8,128)S(1)} %select_bitcast_fusion.2), custom_call_target="InvertDiagBlocksLowerTriangular" | custom-call | tf_op jit(solution)/shard_map/triangular_solve/custom-call.7 | solution.py:123
  324.0 8.8 %custom-call.85 = f32[3,32,32]{2,1,0:T(8,128)S(1)} custom-call(f32[3,32,32]{2,1,0:T(8,128)S(1)} %fusion.85), custom_call_target="Cholesky" | custom-call | tf_op jit(solution)/shard_map/jit(cholesky)/cholesky | solution.py:121
  333.0 7.4 %custom-call.87 = f32[3,1,32,32]{2,3,1,0:T(8,128)S(1)} custom-call(f32[3,1,32,32]{3,2,1,0:T(8,128)S(1)} %select_bitcast_fusion.1), custom_call_target="InvertDiagBlocksLowerTriangular" | custom-call | tf_op jit(solution)/shard_map/triangular_solve/custom-call.7 | solution.py:123
  354.9 5.1 %all-to-all-done.3 = f32[8,65,32]{1,2,0:T(8,128)S(1)} async-done(((f32[8,65,32]{1,2,0:T(8,128)}), f32[8,65,32]{1,2,0:T(8,128)S(1)}, u32[]{:S(2)}, u32[]{:S(2)}) %all-to-all-start.3) | async-done | bytes 66592 | tf_op jit(solution)/shard_map/all_to_all | solution.py:11
  364.2 8.3 %while.15 = (s32[]{:T(128)}, f32[3,8192]{1,0:T(4,128)}, f32[3,32,32]{1,2,0:T(8,128)S(1)}, f32[8192,32]{0,1:T(8,128)S(1)}, s32[]{:T(128)}, /*index=5*/s32[]{:T(128)}) while((s32[]{:T(128)}, f32[3,8192]{1,0:T(4,128)}, f32[3,32,32]{1,2,0:T(8,128)S(1)}, f32[8192,32]{0,1:T(8,128)S(1)}, s32[]{:T(128)}, /*index=5*/s32[]{:T(128)}) %tuple.74), condition=%wide.region_17.26_spmd, body=%wide.region_15.25_spmd.sunk | while | flops 101179392 | bytes 2211925 | solution.py:290
  (464 shorter events, 126.0 us)
Async XLA Ops:
  0.6 70.0 %copy-start = (bf16[8192,64]{0,1:T(8,128)(2,1)S(1)}, bf16[8192,64]{0,1:T(8,128)(2,1)}, u32[]{:S(2)}) copy-start(bf16[8192,64]{0,1:T(8,128)(2,1)} %param.34) | copy-start | bytes 3145732
  29.5 2.3 copy-start.20
  29.5 2.5 copy-start.12
  29.8 2.3 copy-start.13
  29.8 2.3 copy-start.14
  53.3 17.4 %copy-start.9 = (bf16[64,32]{0,1:T(8,128)(2,1)S(1)}, bf16[64,32]{0,1:T(8,128)(2,1)}, u32[]{:S(2)}) copy-start(bf16[64,32]{0,1:T(8,128)(2,1)} %param.35) | copy-start | bytes 12292
  53.3 17.4 %copy-start.16 = (f32[64]{0:T(128)S(1)}, f32[64]{0:T(128)}, u32[]{:S(2)}) copy-start(f32[64]{0:T(128)} %param.36) | copy-start | bytes 772
  58.8 21.8 %all-to-all-start = ((f32[3,32,3,128]{3,2,0,1:T(4,128)}), f32[3,32,3,128]{3,2,0,1:T(4,128)S(1)}, u32[]{:S(2)}, u32[]{:S(2)}) async-start(f32[3,32,3,128]{3,2,0,1:T(4,128)} %bitcast.14), calls=%async_computation | async-start | bytes 393216 | tf_op jit(solution)/shard_map/all_to_all | solution.py:214
  129.5 3.7 copy-start.1
  129.5 11.4 %copy-start.17 = (f32[3]{0:T(128)S(1)}, f32[3]{0:T(128)}, u32[]{:S(2)}) copy-start(f32[3]{0:T(128)} %param.38) | copy-start | bytes 40
  129.5 15.4 %copy-start.10 = (f32[3,32]{1,0:T(4,128)S(1)}, f32[3,32]{1,0:T(4,128)}, u32[]{:S(2)}) copy-start(f32[3,32]{1,0:T(4,128)} %param.37) | copy-start | bytes 1156
  136.3 27.7 %all-to-all-start.1 = ((f32[32,1,7264]{2,1,0:T(1,128)}), f32[32,1,7264]{2,1,0:T(1,128)S(1)}, u32[]{:S(2)}, u32[]{:S(2)}) async-start(f32[32,1,7264]{2,1,0:T(1,128)} %broadcast_in_dim.238), calls=%async_computation.1 | async-start | bytes 1867776 | tf_op jit(solution)/shard_map/all_to_all | solution.py:11
  140.9 8.5 %collective-permute-start.1 = (f32[1]{0:T(128)S(1)}, f32[1]{0:T(128)}, u32[]{:S(2)}, u32[]{:S(2)}) collective-permute-start(f32[1]{0:T(128)S(1)} %bitcast.935), channel_id=1, source_target_pairs={{32,0},{64,32},{96,64},{128,96},{160,128},{192,160},{224,192},{33,... | collective-permute-start | bytes 20 | tf_op jit(solution)/shard_map/ppermute | solution.py:71
  144.9 5.8 %collective-permute-start = (f32[1,32]{1,0:T(1,128)S(1)}, f32[1,32]{1,0:T(1,128)S(1)}, u32[]{:S(2)}, u32[]{:S(2)}) collective-permute-start(f32[1,32]{1,0:T(1,128)S(1)} %slice.588), channel_id=1, source_target_pairs={{32,0},{64,32},{96,64},{128,96},{160,128},{192,160},{224,192},{33,... | collective-permute-start | bytes 392 | tf_op jit(solution)/shard_map/ppermute | solution.py:71
  148.7 67.5 %copy-start.5 = (pred[32,32]{1,0:T(8,128)(4,1)}, pred[32,32]{1,0:T(8,128)(4,1)S(1)}, u32[]{:S(2)}) copy-start(pred[32,32]{1,0:T(8,128)(4,1)S(1)} %iota_compare_fusion.3) | copy-start | bytes 3076
  148.7 67.5 %copy-start.3 = (pred[32,32]{1,0:T(8,128)(4,1)}, pred[32,32]{1,0:T(8,128)(4,1)S(1)}, u32[]{:S(2)}) copy-start(pred[32,32]{1,0:T(8,128)(4,1)S(1)} %iota_compare_fusion.2) | copy-start | bytes 3076
  151.2 83.0 %copy-start.11 = (f32[3,32]{1,0:T(4,128)}, f32[3,32]{1,0:T(4,128)S(1)}, u32[]{:S(2)}) copy-start(f32[3,32]{1,0:T(4,128)S(1)} %get-tuple-element.142) | copy-start | bytes 1156
  239.4 13.2 %all-to-all-start.2 = ((f32[8,98,32]{1,2,0:T(8,128)}), f32[8,98,32]{1,2,0:T(8,128)S(1)}, u32[]{:S(2)}, u32[]{:S(2)}) async-start(f32[8,98,32]{1,2,0:T(8,128)} %broadcast_in_dim.250), calls=%async_computation.2 | async-start | bytes 262144 | tf_op jit(solution)/shard_map/all_to_all | solution.py:11
  248.4 38.1 %copy-start.6 = (pred[32,32]{1,0:T(8,128)(4,1)S(1)}, pred[32,32]{1,0:T(8,128)(4,1)}, u32[]{:S(2)}) copy-start(pred[32,32]{1,0:T(8,128)(4,1)} %copy-done.5) | copy-start | bytes 3076
  252.7 33.8 %copy-start.4 = (pred[32,32]{1,0:T(8,128)(4,1)S(1)}, pred[32,32]{1,0:T(8,128)(4,1)}, u32[]{:S(2)}) copy-start(pred[32,32]{1,0:T(8,128)(4,1)} %copy-done.3) | copy-start | bytes 3076
  253.1 40.0 %copy-start.19 = (pred[8]{0:T(512)(128)(4,1)S(1)}, pred[8]{0:T(512)(128)(4,1)}, u32[]{:S(2)}) copy-start(pred[8]{0:T(512)(128)(4,1)} %iota_compare_fusion.10) | copy-start | bytes 28
  294.2 54.6 %copy-start.15 = (pred[3]{0:T(512)(128)(4,1)S(1)}, pred[3]{0:T(512)(128)(4,1)}, u32[]{:S(2)}) copy-start(pred[3]{0:T(512)(128)(4,1)} %compare_and_fusion) | copy-start | bytes 13
  303.8 56.4 %copy-start.18 = (pred[8]{0:T(512)(128)(4,1)S(1)}, pred[8]{0:T(512)(128)(4,1)}, u32[]{:S(2)}) copy-start(pred[8]{0:T(512)(128)(4,1)} %iota_compare_fusion.9) | copy-start | bytes 28
  350.6 9.4 %all-to-all-start.3 = ((f32[8,65,32]{1,2,0:T(8,128)}), f32[8,65,32]{1,2,0:T(8,128)S(1)}, u32[]{:S(2)}, u32[]{:S(2)}) async-start(f32[8,65,32]{1,2,0:T(8,128)} %broadcast_in_dim.262), calls=%async_computation.3 | async-start | bytes 262144 | tf_op jit(solution)/shard_map/all_to_all | solution.py:11
  (4 other events, 6.1 us)
where the time goes:
time: 375 us; the launch traced here: 374 us
  other arithmetic  173 us (46%)
  local copies, waits for them, and re-layouts  95.8 us (26%)
  matrix products  39.7 us (11%)
  starting transfers between devices  34.6 us (9%)
  waiting for transfers between devices  27.8 us (7%)
    another operation x31, other arithmetic, spd_solve(): lower_chol = jnp.linalg.cholesky(matrix)  68.8 us
    another operation x21, other arithmetic, spd_solve(): lax.linalg.triangular_solve(lower_chol, middle, left_side=True, lower=Tru...  57.7 us
    gather x2, local copies, waits for them, and re-layouts, make_reader(): basis_rows = rows_source[offsets]  48.7 us
    another operation x3, other arithmetic  28 us
    unnamed x62, local copies, waits for them, and re-layouts  26.5 us
    dot_general x112, matrix products, matmul_high(): return jnp.matmul(left_mat, right_mat, precision=HIGHEST)  26.4 us
    all_to_all x3, waiting for transfers between devices, copy_for_each(): lax.all_to_all(jnp.broadcast_to(shard[None], (peers, *shard.shape)), axis...  21.4 us
    all_to_all x3, starting transfers between devices, copy_for_each(): lax.all_to_all(jnp.broadcast_to(shard[None], (peers, *shard.shape)), axis...  16.7 us
  transfers between devices with their start and end apart: 6, of which 4 were waited for; matrix products, arithmetic and copies ran while one was open for 3% of the time, Pallas kernels for 0%

commit v1 on v0

v1 whole, which is shorter than its diff:
```python
import jax
import jax.numpy as jnp
from jax import lax
from jax.experimental import pallas as pl
from jax.experimental.pallas import tpu as pltpu
from jax.sharding import PartitionSpec as P

F32, BF16, I32 = jnp.float32, jnp.bfloat16, jnp.int32
HIGHEST = lax.Precision.HIGHEST
RANK = 32
LANES = 128
PARAMS = pltpu.CompilerParams(vmem_limit_bytes=56 << 20)


def iota(shape, dim):
    return lax.broadcasted_iota(I32, shape, dim)


def nt(a, b):
    return lax.dot_general(a, b, (((1,), (1,)), ((), ())), preferred_element_type=F32)


def nn_high(a, b):
    return lax.dot_general(
        a, b, (((1,), (0,)), ((), ())), precision=HIGHEST, preferred_element_type=F32
    )


def halves(x):
    top = x.astype(BF16).astype(F32)
    return top, x - top


def bucket_kernel(owner_ref, off_ref, val_ref, wgt_ref, bt_ref, send_ref, lhs_s, rt_s):
    days, _, obs = owner_ref.shape
    owners = send_ref.shape[0]
    chunks = obs // LANES
    upper = (iota((LANES, LANES), 0) < iota((LANES, LANES), 1)).astype(F32)
    counter = jnp.concatenate([upper, jnp.ones((LANES, LANES), F32)], axis=1).astype(BF16)
    sub_owner = iota((owners, LANES), 0)
    sub_slot = iota((LANES, LANES), 0)
    for d in range(days):
        base = jnp.zeros((owners, LANES), F32)
        for c in range(chunks):
            at = slice(c * LANES, (c + 1) * LANES)
            hit = sub_owner == owner_ref[d, :, at]
            one_hot = jnp.where(hit, 1.0, 0.0)
            counts = lax.dot_general(
                one_hot.astype(BF16), counter, (((1,), (0,)), ((), ())), preferred_element_type=F32
            )
            slot = jnp.sum(one_hot * (counts[:, :LANES] + base), axis=0, keepdims=True)
            base = base + counts[:, LANES:]
            rt_s[d, :, at] = jnp.where(sub_slot == slot.astype(I32), 1.0, 0.0).astype(BF16)
            weight = wgt_ref[d : d + 1, at]
            offset = off_ref[d : d + 1, at]
            fields = (
                *halves(weight),
                *halves(weight * val_ref[d : d + 1, at]),
                (offset >> 7).astype(F32),
                (offset & 127).astype(F32),
            )
            for f, row in enumerate(fields):
                lhs_s[d, f * owners : (f + 1) * owners, at] = jnp.where(hit, row, 0.0).astype(BF16)
    for d in range(days):
        got = nt(lhs_s[d], rt_s[d])
        part = [got[f * owners : (f + 1) * owners] for f in range(6)]
        for f, x in enumerate((part[0] + part[1], part[2] + part[3], part[4] * 128.0 + part[5])):
            j = f * days + d
            send_ref[:, j * LANES : (j + 1) * LANES] = x
    gram = nt(bt_ref[...], bt_ref[...])
    send_ref[:, 9 * LANES : 10 * LANES] = jnp.concatenate([gram[:32], gram[32:]], axis=1)


def field_kernel(bt_ref, probe_ref, scale_ref, ft_ref, fp_ref):
    scaled = (probe_ref[...].astype(F32) * scale_ref[...]).astype(BF16)
    ft = lax.dot_general(
        scaled, bt_ref[...], (((1,), (0,)), ((), ())), preferred_element_type=F32
    )
    ft_ref[...] = ft
    top = ft.astype(BF16)
    fp_ref[:32] = top
    fp_ref[32:] = (ft - top.astype(F32)).astype(BF16)


def gram_kernel(recv_ref, ft_ref, fp_ref, out_ref, w1_s, w2_s, u1_s, u2_s, off_s, lhs_s, rhs_s, wc_s, uc_s, x_s, pay_s):
    readers = recv_ref.shape[0]
    days = 3
    for d in range(days):
        w = recv_ref[:, d * LANES : (d + 1) * LANES]
        u = recv_ref[:, (3 + d) * LANES : (4 + d) * LANES]
        w1_s[d], w2_s[d] = halves(w)
        u1_s[d], u2_s[d] = halves(u)
        off_s[d] = recv_ref[:, (6 + d) * LANES : (7 + d) * LANES].astype(I32)
    sub64 = iota((64, LANES), 0)
    sub128 = iota((LANES, LANES), 0)

    def spread_reader(r, _):
        at = pl.ds(pl.multiple_of(r * LANES, LANES), LANES)
        for d in range(days):
            offset = off_s[d, pl.ds(r, 1), :]
            hit = sub64 == (offset >> 7)
            for f, ref in enumerate((w1_s, w2_s, u1_s, u2_s)):
                lhs_s[d, f * 64 : (f + 1) * 64, at] = jnp.where(
                    hit, ref[d, pl.ds(r, 1), :], 0.0
                ).astype(BF16)
            rhs_s[d, :, at] = jnp.where(sub128 == (offset & 127), 1.0, 0.0).astype(BF16)
        return 0

    lax.fori_loop(0, readers, spread_reader, 0, unroll=2)
    for d in range(days):
        got = nt(lhs_s[d], rhs_s[d])
        wc_s[d] = got[:64] + got[64:128]
        uc_s[d] = got[128:192] + got[192:]

    def weigh(h, accs):
        at = pl.ds(pl.multiple_of(h * LANES, LANES), LANES)
        ft = ft_ref[:, at]
        new = []
        for d in range(days):
            x = ft * wc_s[d, pl.ds(h, 1), :]
            top = x.astype(BF16)
            x_s[d * 64 : d * 64 + 32, at] = top
            x_s[d * 64 + 32 : d * 64 + 64, at] = (x - top.astype(F32)).astype(BF16)
            new.append(accs[d] + ft * uc_s[d, pl.ds(h, 1), :])
        return tuple(new)

    zero = jnp.zeros((RANK, LANES), F32)
    accs = lax.fori_loop(0, 64, weigh, (zero, zero, zero), unroll=2)
    prod = nt(x_s[...], fp_ref[...])
    chunk = jnp.sum(recv_ref[:, 9 * LANES : 10 * LANES], axis=0, keepdims=True)
    row16, lane16 = iota((16, LANES), 0), iota((16, LANES), 1)
    fold = jnp.where((lane16 >> 3) == row16, chunk, 0.0)
    for shift in (64, 32, 16, 8):
        fold = fold + pltpu.roll(fold, shift, 1)
    pay = jnp.where((lane16 >= 112) & (lane16 < 120), fold, 0.0)
    r16, c16 = iota((16, 16), 0), iota((16, 16), 1)
    pieces = []
    for d in range(days):
        p = prod[d * 64 : (d + 1) * 64]
        sym = p[:32, :32] + p[:32, 32:] + p[32:, :32] + p[32:, 32:]
        low = sym[16:, 16:]
        pieces += [jnp.where(r16 <= c16, sym[:16, :16], low), sym[:16, 16:]]
        diag = jnp.sum(jnp.where(r16 == c16, low, 0.0), axis=1, keepdims=True)
        g = jnp.sum(accs[d], axis=1, keepdims=True)
        pay = jnp.where(lane16 == 96 + 2 * d, g[:16], pay)
        pay = jnp.where(lane16 == 97 + 2 * d, g[16:], pay)
        pay = jnp.where(lane16 == 102 + d, diag, pay)
    pay_s[...] = pay
    for k, piece in enumerate(pieces):
        pay_s[:, 16 * k : 16 * (k + 1)] = piece
    pay = pay_s[...]
    for r in range(readers):
        out_ref[r] = pay


def total_kernel(recv_ref, decay_ref, decay_t_ref, infl_ref, out_ref):
    total = jnp.sum(recv_ref[...], axis=0)
    lane16 = iota((16, LANES), 1)
    lane1 = iota((1, LANES), 1)
    rows = []
    for d in range(3):
        total = jnp.where(lane16 == 105 + 2 * d, decay_t_ref[:16, d : d + 1], total)
        total = jnp.where(lane16 == 106 + 2 * d, decay_t_ref[16:, d : d + 1], total)
    for d in range(3):
        gamma = 1.0 / infl_ref[d]
        dec = decay_ref[d : d + 1, :]
        dec128 = jnp.concatenate([dec, dec, dec, dec], axis=1)
        rows.append(jnp.where(lane1 < 32, gamma, jnp.where(lane1 < 64, -gamma * dec128, 0.0)))
    for d in range(3):
        gamma = 1.0 / infl_ref[d]
        dec = decay_ref[d : d + 1, :]
        dec128 = jnp.concatenate([dec, dec, dec, dec], axis=1)
        rows.append(
            jnp.where(
                lane1 < 32, gamma * dec128, jnp.where((lane1 >= 64) & (lane1 < 96), -gamma, 0.0)
            )
        )
    rows.append(jnp.zeros((2, LANES), F32))
    both = jnp.concatenate([total] + rows, axis=0)
    for r in range(out_ref.shape[0]):
        out_ref[r] = both


def eliminate(mats, want_inv=False):
    sub8 = iota((8, LANES), 0)
    tiles = [[m[8 * t : 8 * t + 8] for t in range(4)] for m in mats]
    over = [[None] * 4 for _ in mats]
    invs = [[None] * 4 for _ in mats]
    for k in range(32):
        q, s = divmod(k, 8)
        for n, a in enumerate(tiles):
            row = jnp.broadcast_to(a[q][s : s + 1, :], (8, LANES))
            inv = 1.0 / jnp.broadcast_to(row[:, k : k + 1], (8, LANES))
            scaled = row * inv
            over[n][q] = scaled if s == 0 else jnp.where(sub8 >= s, scaled, over[n][q])
            if want_inv:
                invs[n][q] = inv if s == 0 else jnp.where(sub8 >= s, inv, invs[n][q])
            for t in range(q, 4):
                if t == q and s == 7:
                    continue
                col = jnp.broadcast_to(a[t][:, k : k + 1], (8, LANES))
                if t == q:
                    col = jnp.where(sub8 > s, col, 0.0)
                a[t] = a[t] - col * scaled
    u = [jnp.concatenate(a, axis=0) for a in tiles]
    v = [jnp.concatenate(a, axis=0) for a in over]
    i = [jnp.concatenate(a, axis=0) for a in invs] if want_inv else None
    return u, v, i


def tn_high(a, b):
    return nn_high(jnp.transpose(a), b)


def setup_kernel(recv_ref, probe_ref, scale_ref, ft_ref, linv_ref, bd_ref, k3_ref, b_ref):
    lane = iota((32, LANES), 1)
    gram = jnp.zeros((32, LANES), F32)
    for i in range(16):
        slab = recv_ref[:, i, :]
        moved = pltpu.roll(slab, (8 * i - 112) % LANES, 1)
        gram = jnp.where((lane >> 3) == i, moved, gram)
    gram = jnp.concatenate([gram[:, :64], gram[:, 64:]], axis=0)
    scale = scale_ref[...]
    scaled = (probe_ref[...].astype(F32) * scale).astype(BF16).astype(F32)
    half = nn_high(scaled, gram)
    core = lax.dot_general(
        half, scaled, (((1,), (1,)), ((), ())), precision=HIGHEST, preferred_element_type=F32
    )
    eye = (iota((32, 32), 0) == iota((32, 32), 1)).astype(F32)
    zero64 = jnp.zeros((32, 64), F32)
    (u,), _, (inv,) = eliminate([jnp.concatenate([core, eye, zero64], axis=1)], want_inv=True)
    linv = u[:, 32:64] * jnp.sqrt(inv[:, :32])
    projected = nn_high(linv, half)
    prior = lax.dot_general(
        projected * (scale * scale),
        projected,
        (((1,), (1,)), ((), ())),
        precision=HIGHEST,
        preferred_element_type=F32,
    )
    (u,), (v,), _ = eliminate([jnp.concatenate([prior, eye, zero64], axis=1)])
    prec = tn_high(v[:, 32:64], u[:, 32:64])
    prec = 0.5 * (prec + jnp.transpose(prec))
    linv_ref[...] = linv
    k3_ref[...] = jnp.concatenate([prec, prec, prec, jnp.zeros((32, 32), F32)], axis=1)
    lt = jnp.transpose(linv)
    zero32 = jnp.zeros((32, 32), F32)
    bd_ref[...] = jnp.concatenate(
        [
            jnp.concatenate([x if i == j else zero32 for j in range(4)], axis=1)
            for i, x in enumerate((lt, lt, lt, eye))
        ],
        axis=0,
    )
    basis = nn_high(linv, ft_ref[...])
    top = basis.astype(BF16)
    b_ref[0:32] = top
    b_ref[32:64] = (basis - top.astype(F32)).astype(BF16)
    b_ref[64:96] = top


class Eliminated:
    def __init__(self, node):
        self.node = node
        self.left = None
        self.right = None


def solve_kernel(pos_ref, recv_ref, linv_ref, bd_ref, k3_ref, b_ref, mean_ref, spread_ref, e_s, x_s):
    lane = iota((32, LANES), 1)
    k3 = k3_ref[...]
    r16, c16 = iota((16, 16), 0), iota((16, 16), 1)
    zero_row = jnp.zeros((1, LANES), F32)
    dcols = []
    for r in range(8):
        x = recv_ref[r, :16, :]
        xt = jnp.transpose(x)
        slabs = []
        for d in range(3):
            a = x[:, 32 * d : 32 * d + 16]
            q = x[:, 32 * d + 16 : 32 * d + 32]
            at = xt[32 * d : 32 * d + 16]
            qt = xt[32 * d + 16 : 32 * d + 32]
            p = jnp.where(r16 <= c16, a, at)
            low = jnp.where(r16 == c16, x[:, 102 + d : 103 + d], jnp.where(r16 > c16, a, at))
            slabs.append(
                jnp.concatenate(
                    [jnp.concatenate([p, q], axis=1), jnp.concatenate([qt, low], axis=1)], axis=0
                )
            )
            dcols.append(
                jnp.concatenate(
                    [x[:, 105 + 2 * d : 106 + 2 * d], x[:, 106 + 2 * d : 107 + 2 * d]], axis=0
                )
            )
        gs = [
            jnp.concatenate([x[:, 96 + 2 * d : 97 + 2 * d], x[:, 97 + 2 * d : 98 + 2 * d]], axis=0)
            for d in range(3)
        ]
        x_s[:, r * LANES : (r + 1) * LANES] = jnp.concatenate(
            slabs + gs + [jnp.zeros((32, 29), F32)], axis=1
        )
    z = nn_high(linv_ref[...], x_s[...])
    zs = jnp.concatenate([z[:, r * LANES : (r + 1) * LANES] for r in range(8)], axis=0)
    hs = nn_high(zs, bd_ref[...])
    first = [recv_ref[b // 3, 16 + b % 3 : 17 + b % 3, :] for b in range(24)]
    first.append(jnp.where(iota((1, LANES), 1) < 32, 1.0, 0.0))
    second = [recv_ref[b // 3, 19 + b % 3 : 20 + b % 3, :] for b in range(24)] + [zero_row]
    dcols.append(jnp.zeros((32, 1), F32))
    for b in range(25):
        nxt = (b + 1) % 25
        e = k3 * first[b] + (k3 * dcols[nxt]) * second[nxt]
        if b < 24:
            h = hs[32 * (b // 3) : 32 * (b // 3) + 32]
            d = b % 3
            mat = h if d == 0 else pltpu.roll(h, LANES - 32 * d, 1)
            vec = h if d == 0 else pltpu.roll(h, LANES - d, 1)
            e = e + jnp.where(lane < 32, mat, jnp.where(lane == 96, vec, 0.0))
        e_s[b] = e
    start = 3 * pos_ref[0]
    nodes = [e_s[lax.rem(start + j, 25)] for j in range(25)]

    plan = [
        {0: [1, 3, 5, 7, 9, 11, 13, 15, 17, 19, 21, 23], 1: [2, 6, 10, 14, 18, 22], 2: [4, 12, 20], 3: [8, 24], 4: [16]},
        {0: [3, 5, 7, 9, 11, 13, 15, 17, 19, 21, 23], 1: [2, 6, 10, 14, 18, 22, 0], 2: [4, 12, 20], 3: [8, 24], 4: [16]},
        {0: [3, 5, 7, 9, 11, 13, 15, 17, 19, 21, 23, 1], 1: [6, 10, 14, 18, 22, 0], 2: [4, 12, 20], 3: [8, 24], 4: [16]},
    ]
    rings = [[(j, j) for j in range(25)] for _ in range(3)]
    values = dict(enumerate(nodes))
    fresh = [25]
    updated = {}

    def renew(key, make):
        if key not in updated:
            values[fresh[0]] = make()
            updated[key] = fresh[0]
            fresh[0] += 1
        return updated[key]

    for level in range(5):
        todo = []
        for target in range(3):
            held = dict(rings[target])
            todo += [held[j] for j in plan[target][level] if held[j] not in todo]
        us, vs, _ = eliminate([values[i] for i in todo])
        prods = {}
        for i, u, v in zip(todo, us, vs):
            prods[i] = nn_high(jnp.transpose(v)[32:96], u)
        for target in range(3):
            ring = rings[target]
            gone = plan[target][level]
            size = len(ring)
            out = []
            for at, (j, i) in enumerate(ring):
                if j in gone:
                    continue
                pj, pi = ring[at - 1]
                nj, ni = ring[(at + 1) % size]
                key = i
                if nj in gone:
                    def as_left(i=i, ni=ni):
                        p = prods[ni][:32]
                        own = jnp.where(lane < 32, pltpu.roll(p, LANES - 32, 1), jnp.where(lane >= 64, p, 0.0))
                        kept = jnp.where((lane < 64) | (lane >= 96), values[i], 0.0)
                        return kept - own

                    i = renew(("l", i, ni), as_left)
                if pj in gone:
                    def as_right(i=i, pi=pi):
                        p = prods[pi][32:]
                        own = jnp.where(
                            lane < 32,
                            pltpu.roll(p, LANES - 64, 1),
                            jnp.where((lane < 64) | (lane >= 96), p, 0.0),
                        )
                        kept = jnp.where((lane < 32) | (lane >= 64), values[i], 0.0)
                        return kept - own

                    i = renew(("r", i, pi), as_right)
                out.append((j, i))
            rings[target] = out
    eye_at = jnp.where(lane == iota((32, LANES), 0) + 32, 1.0, 0.0)
    last = []
    for target in range(3):
        (pair,) = rings[target]
        m = values[pair[1]]
        m = m + jnp.where(lane < 32, pltpu.roll(m, LANES - 32, 1) + pltpu.roll(m, LANES - 64, 1), 0.0)
        last.append(jnp.where((lane < 32) | (lane >= 96), m, 0.0) + eye_at)
    us, vs, _ = eliminate(last)
    rows, sums = [], []
    for u, v in zip(us, vs):
        vt = jnp.transpose(v)
        cov = nn_high(vt[32:64], u)[:, 32:64]
        rows.append(cov)
        sums.append(nn_high(vt[96:104], u)[0:1, 32:64])
    lhs = jnp.concatenate(rows + sums + [jnp.zeros((5, 32), F32)], axis=0)
    one, two = halves(lhs)
    lhs = jnp.concatenate([one, one, two], axis=1).astype(BF16)
    cells = b_ref.shape[1]
    step = 512

    def finish(c, _):
        at = pl.ds(pl.multiple_of(c * step, step), step)
        b = b_ref[:, at]
        y = lax.dot_general(lhs, b, (((1,), (0,)), ((), ())), preferred_element_type=F32)
        wide = b[0:32].astype(F32) + b[32:64].astype(F32)
        for d in range(3):
            spread_ref[d : d + 1, at] = jnp.sum(y[32 * d : 32 * d + 32] * wide, axis=0, keepdims=True)
            mean_ref[d : d + 1, at] = y[96 + d : 97 + d]
        return 0

    lax.fori_loop(0, cells // step, finish, 0, unroll=2)


def shape(*dims, dtype=F32):
    return jax.ShapeDtypeStruct(dims, dtype)


def call(kernel, out, scratch=(), in_specs=None, name=None):
    extra = {} if in_specs is None else {"in_specs": in_specs}
    return pl.pallas_call(
        kernel, out_shape=out, scratch_shapes=list(scratch), compiler_params=PARAMS, name=name, **extra
    )


VM = pl.BlockSpec(memory_space=pltpu.VMEM)
SM = pl.BlockSpec(memory_space=pltpu.SMEM)


def body(
    background, probe, member_scale, decay, inflation, obs_owner, obs_offset, obs_value, obs_weight
):
    bt = background.T
    probe_t = probe.T
    scale = member_scale.reshape(1, -1)
    owner = obs_owner.transpose(0, 2, 1)
    cells = bt.shape[1]
    send = call(
        bucket_kernel,
        shape(32, 1280),
        [pltpu.VMEM((3, 192, 2048), BF16), pltpu.VMEM((3, 128, 2048), BF16)],
        name="buckets",
    )(owner, obs_offset, obs_value, obs_weight, bt)
    recv = lax.all_to_all(send, "space", 0, 0, tiled=True)
    ft, fp = call(
        field_kernel, (shape(32, cells), shape(64, cells, dtype=BF16)), name="field"
    )(bt, probe_t, scale)
    payload = call(
        gram_kernel,
        shape(32, 16, 128),
        [
            pltpu.VMEM((3, 32, 128), F32),
            pltpu.VMEM((3, 32, 128), F32),
            pltpu.VMEM((3, 32, 128), F32),
            pltpu.VMEM((3, 32, 128), F32),
            pltpu.VMEM((3, 32, 128), I32),
            pltpu.VMEM((3, 256, 4096), BF16),
            pltpu.VMEM((3, 128, 4096), BF16),
            pltpu.VMEM((3, 64, 128), F32),
            pltpu.VMEM((3, 64, 128), F32),
            pltpu.VMEM((192, cells), BF16),
            pltpu.VMEM((16, 128), F32),
        ],
        name="grams",
    )(recv, ft, fp)
    recv_2 = lax.all_to_all(payload, "space", 0, 0, tiled=True)
    both = call(total_kernel, shape(8, 24, 128), in_specs=[VM, VM, VM, SM], name="totals")(
        recv_2, decay, decay.T, inflation
    )
    recv_3 = lax.all_to_all(both, "tm", 0, 0, tiled=True)
    linv, bd, k3, basis = call(
        setup_kernel,
        (shape(32, 32), shape(128, 128), shape(32, 128), shape(96, cells, dtype=BF16)),
        name="setup",
    )(recv_2, probe_t, scale, ft)
    pos = lax.axis_index("tm").astype(I32).reshape(1)
    mean, spread = call(
        solve_kernel,
        (shape(3, cells), shape(3, cells)),
        [pltpu.VMEM((25, 32, 128), F32), pltpu.VMEM((32, 1024), F32)],
        in_specs=[SM, VM, VM, VM, VM, VM],
        name="solve",
    )(pos, recv_3, linv, bd, k3, basis)
    return mean, spread


def solution(mesh):
    return jax.shard_map(
        body,
        mesh=mesh,
        in_specs=(
            P("space", None),
            P(),
            P(),
            P("tm", None),
            P("tm"),
            P("tm", "space", None),
            P("tm", "space"),
            P("tm", "space"),
            P("tm", "space"),
        ),
        out_specs=(P("tm", "space"), P("tm", "space")),
        check_vma=False,
    )
```

time: 375 us -> 112 us (0.30)
  other arithmetic: 173 us -> 0 us
  local copies, waits for them, and re-layouts: 95.8 us -> 4.47 us
  Pallas kernels: 0 us -> 66 us
  matrix products: 39.7 us -> 0 us
  waiting for transfers between devices: 27.8 us -> 16.4 us
  starting transfers between devices: 34.6 us -> 24.2 us
    another operation x62 -> x0, other arithmetic: 161 us -> none  [the longest x31 68.8 us: spd_solve(): lower_chol = jnp.linalg.cholesky(matrix)]
    pallas_call x0 -> x6, Pallas kernels: none -> 66 us  [the longest x1 33.4 us: body(): call(solve_kernel, (shape(3, cells), shape(3, cells)), [pltpu.VMEM((25, 3...]
    gather x2 -> x0, local copies, waits for them, and re-layouts: 48.7 us -> none  [make_reader(): basis_rows = rows_source[offsets]]
    dot_general x116 -> x0, matrix products: 32.3 us -> none  [the longest x112 26.4 us: matmul_high(): return jnp.matmul(left_mat, right_mat, precision=HIGHEST)]
    unnamed x62 -> x8, local copies, waits for them, and re-layouts: 26.5 us -> 2.71 us
    all_to_all x4 -> x3, waiting for transfers between devices: 27.8 us -> 16.4 us  [the longest x1 9.7 us: body(): recv_2 = lax.all_to_all(payload, 'space', 0, 0, tiled=True)]
    another operation x26 -> x0, matrix products: 7.17 us -> none  [the longest x10 4.03 us: spd_solve(): lax.linalg.triangular_solve(lower_chol, right_side, left_side=True, lower...]
    ppermute x2 -> x0, starting transfers between devices: 6.06 us -> none  [passed_along(): lax.ppermute(value, axis, [(source, source + steps) for source in range(i...]
  transfers between devices with their start and end apart: 6 -> 3, of which waited for: 4 -> 2; matrix products, arithmetic and copies ran while one was open for 3% -> 1% of each run, Pallas kernels for 0% -> 14%
where the time goes in v1:
time: 112 us
  Pallas kernels  66 us (59%)
  starting transfers between devices  24.2 us (22%)
  waiting for transfers between devices  16.4 us (15%)
  local copies, waits for them, and re-layouts  4.47 us (4%)
    pallas_call x1, Pallas kernels, body(): call(solve_kernel, (shape(3, cells), shape(3, cells)), [pltpu.VMEM((25, 3...  33.4 us
    pallas_call x1, Pallas kernels, body(): call(setup_kernel, (shape(32, 32), shape(128, 128), shape(32, 128), shape...  12.5 us
    all_to_all x1, starting transfers between devices, body(): recv = lax.all_to_all(send, 'space', 0, 0, tiled=True)  11.9 us
    pallas_call x1, Pallas kernels, body(): call(gram_kernel, shape(32, 16, 128), [pltpu.VMEM((3, 32, 128), F32), plt...  11.5 us
    all_to_all x1, waiting for transfers between devices, body(): recv_2 = lax.all_to_all(payload, 'space', 0, 0, tiled=True)  9.7 us
    all_to_all x1, starting transfers between devices, body(): recv_3 = lax.all_to_all(both, 'tm', 0, 0, tiled=True)  8.23 us
    all_to_all x1, waiting for transfers between devices, body(): recv = lax.all_to_all(send, 'space', 0, 0, tiled=True)  6.72 us
    all_to_all x1, starting transfers between devices, body(): recv_2 = lax.all_to_all(payload, 'space', 0, 0, tiled=True)  4.13 us
  transfers between devices with their start and end apart: 3, of which 2 were waited for; matrix products, arithmetic and copies ran while one was open for 1% of the time, Pallas kernels for 14%

profile of v1, /device:TPU:1, one launch (start us, length us, event | category | flops | bytes accessed | tf_op | source)
XLA Modules:
  0.0 111.7 jit_solution(17822267376874399455)
XLA Ops:
  0.6 4.0 %buckets.1 = f32[32,1280]{1,0:T(8,128)} custom-call(s32[3,1,2048]{2,1,0:T(1,128)} %bitcast.17, s32[3,2048]{1,0:T(4,128)} %off_ref.1, f32[3,2048]{1,0:T(4,128)} %val_ref.1, f32[3,2048]{1,0:T(4,128)} %wgt_ref.1, bf16[64,8192]{1,0:T(8,128)(2,1)} %bitcast.10), custom_call_target="tpu_custom_call" | custom-call | tf_op jit(solution)/shard_map/buckets/pallas_call | solution.py:438
  4.6 1.8 %copy.12 = f32[32,1,1280]{2,1,0:T(1,128)} copy(f32[32,1,1280]{2,0,1:T(8,128)} %bitcast.13) | data formatting | bytes 327680 | tf_op jit(solution)/shard_map/all_to_all | solution.py:444
  6.4 11.9 %all-to-all-start = ((f32[32,1,1280]{2,1,0:T(1,128)}), f32[32,1,1280]{2,1,0:T(1,128)S(1)}, u32[]{:S(2)}, u32[]{:S(2)}) async-start(f32[32,1,1280]{2,1,0:T(1,128)} %copy.12), calls=%async_computation | async-start | bytes 327680 | tf_op jit(solution)/shard_map/all_to_all | solution.py:444
  18.2 2.9 %field.1 = (f32[32,8192]{1,0:T(8,128)}, bf16[64,8192]{1,0:T(8,128)(2,1)}) custom-call(bf16[64,8192]{1,0:T(8,128)(2,1)} %bitcast.11, bf16[32,64]{1,0:T(8,128)(2,1)} %bitcast.15, f32[1,64]{1,0:T(1,128)} %bitcast.18), custom_call_target="tpu_custom_call" | custom-call | tf_op jit(solution)/shard_map/field/pallas_call | solution.py:445
  21.1 6.7 %all-to-all-done = f32[32,1,1280]{2,1,0:T(1,128)S(1)} async-done(((f32[32,1,1280]{2,1,0:T(1,128)}), f32[32,1,1280]{2,1,0:T(1,128)S(1)}, u32[]{:S(2)}, u32[]{:S(2)}) %all-to-all-start) | async-done | bytes 163872 | tf_op jit(solution)/shard_map/all_to_all | solution.py:444
  27.8 0.7 copy.16
  28.5 0.0 copy-start.2
  28.5 11.5 %grams.1 = f32[32,16,128]{2,1,0:T(8,128)} custom-call(f32[32,1280]{1,0:T(8,128)} %bitcast.12, f32[32,8192]{1,0:T(8,128)} %get-tuple-element.8.ft_ref, bf16[64,8192]{1,0:T(8,128)(2,1)} %get-tuple-element.9.fp_ref), custom_call_target="tpu_custom_call" | custom-call | tf_op jit(solution)/shard_map/grams/pallas_call | solution.py:448
  40.0 4.1 %all-to-all-start.1 = ((f32[32,16,128]{2,1,0:T(8,128)}), f32[32,16,128]{2,1,0:T(8,128)S(1)}, u32[]{:S(2)}, u32[]{:S(2)}) async-start(f32[32,16,128]{2,1,0:T(8,128)} %grams.1), calls=%async_computation.1 | async-start | bytes 524288 | tf_op jit(solution)/shard_map/all_to_all | solution.py:466
  44.2 0.0 copy-done.2
  44.2 0.7 copy.13
  44.9 9.7 %all-to-all-done.1.recv_ref = f32[32,16,128]{2,1,0:T(8,128)S(1)} async-done(((f32[32,16,128]{2,1,0:T(8,128)}), f32[32,16,128]{2,1,0:T(8,128)S(1)}, u32[]{:S(2)}, u32[]{:S(2)}) %all-to-all-start.1) | async-done | bytes 262176 | tf_op jit(solution)/shard_map/all_to_all | solution.py:466
  54.6 0.0 copy-start
  54.6 0.7 copy-done
  55.3 1.7 %totals.1 = f32[8,24,128]{2,1,0:T(8,128)} custom-call(f32[32,16,128]{2,1,0:T(8,128)} %copy-done, f32[3,32]{1,0:T(4,128)} %decay_ref.1, f32[32,3]{1,0:T(8,128)} %bitcast.14, f32[3]{0:T(128)} %infl_ref.1), custom_call_target="tpu_custom_call" | custom-call | tf_op jit(solution)/shard_map/totals/pallas_call | solution.py:467
  57.0 8.2 %all-to-all-start.2 = ((f32[8,24,128]{2,1,0:T(8,128)}), f32[8,24,128]{2,1,0:T(8,128)S(1)}, u32[]{:S(2)}, u32[]{:S(2)}) async-start(f32[8,24,128]{2,1,0:T(8,128)} %totals.1), calls=%async_computation.2 | async-start | bytes 196608 | tf_op jit(solution)/shard_map/all_to_all | solution.py:470
  65.2 12.5 %setup.1 = (f32[32,32]{1,0:T(8,128)}, f32[128,128]{1,0:T(8,128)}, f32[32,128]{1,0:T(8,128)}, bf16[96,8192]{1,0:T(8,128)(2,1)}) custom-call(f32[32,16,128]{2,1,0:T(8,128)} %copy-done, bf16[32,64]{1,0:T(8,128)(2,1)} %bitcast.16, f32[1,64]{1,0:T(1,128)} %bitcast.19, f32[32,8192]{1,0:T(8,128)} %get-tuple-element.8.ft_ref), custom_call_target="tpu_custom_call" | custom-call | tf_op jit(solution)/shard_map/setup/pallas_call | solution.py:471
  77.7 0.0 all-to-all-done.2.recv_ref
  77.7 0.0 copy-start.1
  77.7 0.7 copy-done.1
  78.4 33.4 %solve.1 = (f32[3,8192]{1,0:T(4,128)}, f32[3,8192]{1,0:T(4,128)}) custom-call(s32[1]{0:T(128)} %bitcast.pos_ref, f32[8,24,128]{2,1,0:T(8,128)} %copy-done.1, f32[32,32]{1,0:T(8,128)} %get-tuple-element.10.linv_ref, f32[128,128]{1,0:T(8,128)} %get-tuple-element.11.bd_ref, f32[32,128]{1,0:T(8,128)} %get-tuple-element.12.k3_ref, ...), custom_call_target="tpu_custom_call" | custom-call | tf_op jit(solution)/shard_map/solve/pallas_call | solution.py:477
Async XLA Ops:
  6.4 21.5 %all-to-all-start = ((f32[32,1,1280]{2,1,0:T(1,128)}), f32[32,1,1280]{2,1,0:T(1,128)S(1)}, u32[]{:S(2)}, u32[]{:S(2)}) async-start(f32[32,1,1280]{2,1,0:T(1,128)} %copy.12), calls=%async_computation | async-start | bytes 327680 | tf_op jit(solution)/shard_map/all_to_all | solution.py:444
  28.5 15.7 %copy-start.2 = (f32[3,32]{1,0:T(4,128)S(1)}, f32[3,32]{1,0:T(4,128)}, u32[]{:S(2)}) copy-start(f32[3,32]{1,0:T(4,128)} %decay_ref.1) | copy-start | bytes 1156
  40.0 14.5 %all-to-all-start.1 = ((f32[32,16,128]{2,1,0:T(8,128)}), f32[32,16,128]{2,1,0:T(8,128)S(1)}, u32[]{:S(2)}, u32[]{:S(2)}) async-start(f32[32,16,128]{2,1,0:T(8,128)} %grams.1), calls=%async_computation.1 | async-start | bytes 524288 | tf_op jit(solution)/shard_map/all_to_all | solution.py:466
  54.6 0.7 copy-start
  57.0 20.7 %all-to-all-start.2 = ((f32[8,24,128]{2,1,0:T(8,128)}), f32[8,24,128]{2,1,0:T(8,128)S(1)}, u32[]{:S(2)}, u32[]{:S(2)}) async-start(f32[8,24,128]{2,1,0:T(8,128)} %totals.1), calls=%async_computation.2 | async-start | bytes 196608 | tf_op jit(solution)/shard_map/all_to_all | solution.py:470
  77.7 0.7 copy-start.1

commit v2 on v1

--- a/solution.py
+++ b/solution.py
@@ -66,9 +66,9 @@
         part = [got[f * owners : (f + 1) * owners] for f in range(6)]
         for f, x in enumerate((part[0] + part[1], part[2] + part[3], part[4] * 128.0 + part[5])):
             j = f * days + d
-            send_ref[:, j * LANES : (j + 1) * LANES] = x
+            send_ref[:, 0, j * LANES : (j + 1) * LANES] = x
     gram = nt(bt_ref[...], bt_ref[...])
-    send_ref[:, 9 * LANES : 10 * LANES] = jnp.concatenate([gram[:32], gram[32:]], axis=1)
+    send_ref[:, 0, 9 * LANES : 10 * LANES] = jnp.concatenate([gram[:32], gram[32:]], axis=1)
 
 
 def field_kernel(bt_ref, probe_ref, scale_ref, ft_ref, fp_ref):
@@ -78,56 +78,52 @@
     )
     ft_ref[...] = ft
     top = ft.astype(BF16)
-    fp_ref[:32] = top
-    fp_ref[32:] = (ft - top.astype(F32)).astype(BF16)
-
-
-def gram_kernel(recv_ref, ft_ref, fp_ref, out_ref, w1_s, w2_s, u1_s, u2_s, off_s, lhs_s, rhs_s, wc_s, uc_s, x_s, pay_s):
+    fp_ref[0:32] = top
+    fp_ref[32:64] = (ft - top.astype(F32)).astype(BF16)
+    fp_ref[64:96] = top
+
+
+def gram_kernel(recv_ref, ft_ref, fp_ref, out_ref, lhs_s, rhs_s, wc_s, uc_s, pay_s):
     readers = recv_ref.shape[0]
     days = 3
+    sub64 = iota((64, LANES), 0).astype(F32).astype(BF16)
+    sub128 = iota((LANES, LANES), 0).astype(F32).astype(BF16)
+    zero = jnp.zeros((), BF16)
+
+    def packed(x, r, rows):
+        line = jnp.broadcast_to(x[r : r + 1], (16, LANES)).astype(BF16)
+        return jnp.concatenate([line] * (rows // 16), axis=0)
+
     for d in range(days):
-        w = recv_ref[:, d * LANES : (d + 1) * LANES]
-        u = recv_ref[:, (3 + d) * LANES : (4 + d) * LANES]
-        w1_s[d], w2_s[d] = halves(w)
-        u1_s[d], u2_s[d] = halves(u)
-        off_s[d] = recv_ref[:, (6 + d) * LANES : (7 + d) * LANES].astype(I32)
-    sub64 = iota((64, LANES), 0)
-    sub128 = iota((LANES, LANES), 0)
-
-    def spread_reader(r, _):
-        at = pl.ds(pl.multiple_of(r * LANES, LANES), LANES)
-        for d in range(days):
-            offset = off_s[d, pl.ds(r, 1), :]
-            hit = sub64 == (offset >> 7)
-            for f, ref in enumerate((w1_s, w2_s, u1_s, u2_s)):
-                lhs_s[d, f * 64 : (f + 1) * 64, at] = jnp.where(
-                    hit, ref[d, pl.ds(r, 1), :], 0.0
-                ).astype(BF16)
-            rhs_s[d, :, at] = jnp.where(sub128 == (offset & 127), 1.0, 0.0).astype(BF16)
-        return 0
-
-    lax.fori_loop(0, readers, spread_reader, 0, unroll=2)
-    for d in range(days):
+        w = halves(recv_ref[:, 0, d * LANES : (d + 1) * LANES])
+        u = halves(recv_ref[:, 0, (3 + d) * LANES : (4 + d) * LANES])
+        offset = recv_ref[:, 0, (6 + d) * LANES : (7 + d) * LANES].astype(I32)
+        high, low = (offset >> 7).astype(F32), (offset & 127).astype(F32)
+        for r in range(readers):
+            at = slice(r * LANES, (r + 1) * LANES)
+            hit = sub64 == packed(high, r, 64)
+            for f, x in enumerate(w + u):
+                lhs_s[d, f * 64 : (f + 1) * 64, at] = jnp.where(hit, packed(x, r, 64), zero)
+            rhs_s[d, :, at] = jnp.where(sub128 == packed(low, r, LANES), jnp.ones((), BF16), zero)
         got = nt(lhs_s[d], rhs_s[d])
         wc_s[d] = got[:64] + got[64:128]
         uc_s[d] = got[128:192] + got[192:]
-
-    def weigh(h, accs):
-        at = pl.ds(pl.multiple_of(h * LANES, LANES), LANES)
-        ft = ft_ref[:, at]
-        new = []
-        for d in range(days):
-            x = ft * wc_s[d, pl.ds(h, 1), :]
-            top = x.astype(BF16)
-            x_s[d * 64 : d * 64 + 32, at] = top
-            x_s[d * 64 + 32 : d * 64 + 64, at] = (x - top.astype(F32)).astype(BF16)
-            new.append(accs[d] + ft * uc_s[d, pl.ds(h, 1), :])
-        return tuple(new)
-
-    zero = jnp.zeros((RANK, LANES), F32)
-    accs = lax.fori_loop(0, 64, weigh, (zero, zero, zero), unroll=2)
-    prod = nt(x_s[...], fp_ref[...])
-    chunk = jnp.sum(recv_ref[:, 9 * LANES : 10 * LANES], axis=0, keepdims=True)
+    accs = [jnp.zeros((RANK, LANES), F32)] * days
+    prod = jnp.zeros((days * 64, 64), F32)
+    for start in range(0, 64, 4):
+        xs = []
+        for h in range(start, start + 4):
+            ft = ft_ref[:, h * LANES : (h + 1) * LANES]
+            pieces = []
+            for d in range(days):
+                x = ft * wc_s[d, h : h + 1, :]
+                top = x.astype(BF16)
+                pieces += [top, (x - top.astype(F32)).astype(BF16)]
+                accs[d] = accs[d] + ft * uc_s[d, h : h + 1, :]
+            xs.append(jnp.concatenate(pieces, axis=0))
+        x = jnp.concatenate(xs, axis=1)
+        prod = prod + nt(x, fp_ref[0:64, start * LANES : (start + 4) * LANES])
+    chunk = jnp.sum(recv_ref[:, 0, 9 * LANES : 10 * LANES], axis=0, keepdims=True)
     row16, lane16 = iota((16, LANES), 0), iota((16, LANES), 1)
     fold = jnp.where((lane16 >> 3) == row16, chunk, 0.0)
     for shift in (64, 32, 16, 8):
@@ -181,38 +177,79 @@
         out_ref[r] = both
 
 
-def eliminate(mats, want_inv=False):
+def eliminate(mats):
     sub8 = iota((8, LANES), 0)
+    low = sub8 >= 4
     tiles = [[m[8 * t : 8 * t + 8] for t in range(4)] for m in mats]
     over = [[None] * 4 for _ in mats]
-    invs = [[None] * 4 for _ in mats]
-    for k in range(32):
+    wide = lambda x: jnp.broadcast_to(x, (8, LANES))
+    for k in range(0, 32, 4):
         q, s = divmod(k, 8)
         for n, a in enumerate(tiles):
-            row = jnp.broadcast_to(a[q][s : s + 1, :], (8, LANES))
-            inv = 1.0 / jnp.broadcast_to(row[:, k : k + 1], (8, LANES))
-            scaled = row * inv
-            over[n][q] = scaled if s == 0 else jnp.where(sub8 >= s, scaled, over[n][q])
-            if want_inv:
-                invs[n][q] = inv if s == 0 else jnp.where(sub8 >= s, inv, invs[n][q])
+            r = [wide(a[q][s + i : s + i + 1, :]) for i in range(4)]
+            m = {(i, j): wide(r[i][:, k + j : k + j + 1]) for i in range(4) for j in range(i, 4)}
+            ia = 1.0 / (m[0, 0] * m[1, 1] - m[0, 1] * m[0, 1])
+            x02 = (m[1, 1] * m[0, 2] - m[0, 1] * m[1, 2]) * ia
+            x03 = (m[1, 1] * m[0, 3] - m[0, 1] * m[1, 3]) * ia
+            x12 = (m[0, 0] * m[1, 2] - m[0, 1] * m[0, 2]) * ia
+            x13 = (m[0, 0] * m[1, 3] - m[0, 1] * m[0, 3]) * ia
+            s22 = m[2, 2] - m[0, 2] * x02 - m[1, 2] * x12
+            s23 = m[2, 3] - m[0, 2] * x03 - m[1, 2] * x13
+            s33 = m[3, 3] - m[0, 3] * x03 - m[1, 3] * x13
+            ib = 1.0 / (s22 * s33 - s23 * s23)
+            t0 = (m[1, 1] * r[0] - m[0, 1] * r[1]) * ia
+            t1 = (m[0, 0] * r[1] - m[0, 1] * r[0]) * ia
+            z2 = r[2] - x02 * r[0] - x12 * r[1]
+            z3 = r[3] - x03 * r[0] - x13 * r[1]
+            v2 = (s33 * z2 - s23 * z3) * ib
+            v3 = (s22 * z3 - s23 * z2) * ib
+            v0 = t0 - x02 * v2 - x03 * v3
+            v1 = t1 - x12 * v2 - x13 * v3
+            v = (v0, v1, v2, v3)
+            got = v0
+            for i in (1, 2, 3):
+                got = jnp.where(sub8 >= s + i, v[i], got)
+            over[n][q] = got if s == 0 else jnp.where(low, got, over[n][q])
             for t in range(q, 4):
-                if t == q and s == 7:
+                if t == q and s == 4:
                     continue
-                col = jnp.broadcast_to(a[t][:, k : k + 1], (8, LANES))
+                c = [wide(a[t][:, k + i : k + i + 1]) for i in range(4)]
+                delta = (c[0] * v0 + c[1] * v1) + (c[2] * v2 + c[3] * v3)
                 if t == q:
-                    col = jnp.where(sub8 > s, col, 0.0)
-                a[t] = a[t] - col * scaled
+                    delta = jnp.where(low, delta, 0.0)
+                a[t] = a[t] - delta
     u = [jnp.concatenate(a, axis=0) for a in tiles]
     v = [jnp.concatenate(a, axis=0) for a in over]
-    i = [jnp.concatenate(a, axis=0) for a in invs] if want_inv else None
-    return u, v, i
+    return u, v
+
+
+def finish_factor(u):
+    sub8 = iota((8, LANES), 0)
+    low = sub8 < 4
+    within = sub8 & 3
+    wide = lambda x: jnp.broadcast_to(x, (8, LANES))
+    out = []
+    for t in range(4):
+        a = u[8 * t : 8 * t + 8]
+        scale = jnp.zeros((8, LANES), F32)
+        for i in range(4):
+            row = jnp.where(low, wide(a[i : i + 1]), wide(a[4 + i : 5 + i]))
+            at = 8 * t + i
+            pivot = jnp.where(low, wide(row[:, at : at + 1]), wide(row[:, at + 4 : at + 5]))
+            inv = 1.0 / pivot
+            scale = jnp.where(within == i, jnp.sqrt(inv), scale)
+            if i < 3:
+                col = jnp.where(low, wide(a[:, at : at + 1]), wide(a[:, at + 4 : at + 5]))
+                a = a - jnp.where(within > i, col * (row * inv), 0.0)
+        out.append(a * scale)
+    return jnp.concatenate(out, axis=0)
 
 
 def tn_high(a, b):
     return nn_high(jnp.transpose(a), b)
 
 
-def setup_kernel(recv_ref, probe_ref, scale_ref, ft_ref, linv_ref, bd_ref, k3_ref, b_ref):
+def setup_kernel(recv_ref, probe_ref, scale_ref, fp_ref, linv_ref, bd_ref, k3_ref, b_ref):
     lane = iota((32, LANES), 1)
     gram = jnp.zeros((32, LANES), F32)
     for i in range(16):
@@ -228,8 +265,8 @@
     )
     eye = (iota((32, 32), 0) == iota((32, 32), 1)).astype(F32)
     zero64 = jnp.zeros((32, 64), F32)
-    (u,), _, (inv,) = eliminate([jnp.concatenate([core, eye, zero64], axis=1)], want_inv=True)
-    linv = u[:, 32:64] * jnp.sqrt(inv[:, :32])
+    (u,), _ = eliminate([jnp.concatenate([core, eye, zero64], axis=1)])
+    linv = finish_factor(u)[:, 32:64]
     projected = nn_high(linv, half)
     prior = lax.dot_general(
         projected * (scale * scale),
@@ -238,7 +275,7 @@
         precision=HIGHEST,
         preferred_element_type=F32,
     )
-    (u,), (v,), _ = eliminate([jnp.concatenate([prior, eye, zero64], axis=1)])
+    (u,), (v,) = eliminate([jnp.concatenate([prior, eye, zero64], axis=1)])
     prec = tn_high(v[:, 32:64], u[:, 32:64])
     prec = 0.5 * (prec + jnp.transpose(prec))
     linv_ref[...] = linv
@@ -252,18 +289,17 @@
         ],
         axis=0,
     )
-    basis = nn_high(linv, ft_ref[...])
+    one, two = halves(linv)
+    basis = lax.dot_general(
+        jnp.concatenate([one, one, two], axis=1).astype(BF16),
+        fp_ref[...],
+        (((1,), (0,)), ((), ())),
+        preferred_element_type=F32,
+    )
     top = basis.astype(BF16)
     b_ref[0:32] = top
     b_ref[32:64] = (basis - top.astype(F32)).astype(BF16)
     b_ref[64:96] = top
-
-
-class Eliminated:
-    def __init__(self, node):
-        self.node = node
-        self.left = None
-        self.right = None
 
 
 def solve_kernel(pos_ref, recv_ref, linv_ref, bd_ref, k3_ref, b_ref, mean_ref, spread_ref, e_s, x_s):
@@ -342,7 +378,7 @@
         for target in range(3):
             held = dict(rings[target])
             todo += [held[j] for j in plan[target][level] if held[j] not in todo]
-        us, vs, _ = eliminate([values[i] for i in todo])
+        us, vs = eliminate([values[i] for i in todo])
         prods = {}
         for i, u, v in zip(todo, us, vs):
             prods[i] = nn_high(jnp.transpose(v)[32:96], u)
@@ -386,7 +422,7 @@
         m = values[pair[1]]
         m = m + jnp.where(lane < 32, pltpu.roll(m, LANES - 32, 1) + pltpu.roll(m, LANES - 64, 1), 0.0)
         last.append(jnp.where((lane < 32) | (lane >= 96), m, 0.0) + eye_at)
-    us, vs, _ = eliminate(last)
+    us, vs = eliminate(last)
     rows, sums = [], []
     for u, v in zip(us, vs):
         vt = jnp.transpose(v)
@@ -416,6 +452,10 @@
     return jax.ShapeDtypeStruct(dims, dtype)
 
 
+def on_chip(*xs):
+    return tuple(pltpu.with_memory_space_constraint(x, pltpu.VMEM) for x in xs)
+
+
 def call(kernel, out, scratch=(), in_specs=None, name=None):
     extra = {} if in_specs is None else {"in_specs": in_specs}
     return pl.pallas_call(
@@ -437,42 +477,45 @@
     cells = bt.shape[1]
     send = call(
         bucket_kernel,
-        shape(32, 1280),
+        pltpu.VMEM((32, 1, 1280), F32),
         [pltpu.VMEM((3, 192, 2048), BF16), pltpu.VMEM((3, 128, 2048), BF16)],
         name="buckets",
     )(owner, obs_offset, obs_value, obs_weight, bt)
     recv = lax.all_to_all(send, "space", 0, 0, tiled=True)
     ft, fp = call(
-        field_kernel, (shape(32, cells), shape(64, cells, dtype=BF16)), name="field"
+        field_kernel, (pltpu.VMEM((32, cells), F32), pltpu.VMEM((96, cells), BF16)), name="field"
     )(bt, probe_t, scale)
+    recv, ft, fp = on_chip(recv, ft, fp)
     payload = call(
         gram_kernel,
-        shape(32, 16, 128),
+        pltpu.VMEM((32, 16, 128), F32),
         [
-            pltpu.VMEM((3, 32, 128), F32),
-            pltpu.VMEM((3, 32, 128), F32),
-            pltpu.VMEM((3, 32, 128), F32),
-            pltpu.VMEM((3, 32, 128), F32),
-            pltpu.VMEM((3, 32, 128), I32),
             pltpu.VMEM((3, 256, 4096), BF16),
             pltpu.VMEM((3, 128, 4096), BF16),
             pltpu.VMEM((3, 64, 128), F32),
             pltpu.VMEM((3, 64, 128), F32),
-            pltpu.VMEM((192, cells), BF16),
             pltpu.VMEM((16, 128), F32),
         ],
         name="grams",
     )(recv, ft, fp)
     recv_2 = lax.all_to_all(payload, "space", 0, 0, tiled=True)
-    both = call(total_kernel, shape(8, 24, 128), in_specs=[VM, VM, VM, SM], name="totals")(
+    (recv_2,) = on_chip(recv_2)
+    both = call(total_kernel, pltpu.VMEM((8, 24, 128), F32), in_specs=[VM, VM, VM, SM], name="totals")(
         recv_2, decay, decay.T, inflation
     )
     recv_3 = lax.all_to_all(both, "tm", 0, 0, tiled=True)
+    (recv_3,) = on_chip(recv_3)
     linv, bd, k3, basis = call(
         setup_kernel,
-        (shape(32, 32), shape(128, 128), shape(32, 128), shape(96, cells, dtype=BF16)),
+        (
+            pltpu.VMEM((32, 32), F32),
+            pltpu.VMEM((128, 128), F32),
+            pltpu.VMEM((32, 128), F32),
+            pltpu.VMEM((96, cells), BF16),
+        ),
         name="setup",
-    )(recv_2, probe_t, scale, ft)
+    )(recv_2, probe_t, scale, fp)
+    linv, bd, k3, basis = on_chip(linv, bd, k3, basis)
     pos = lax.axis_index("tm").astype(I32).reshape(1)
     mean, spread = call(
         solve_kernel,

time: 112 us -> 83.2 us (0.74)
  Pallas kernels: 66 us -> 37.9 us
  local copies, waits for them, and re-layouts: 4.47 us -> 2.16 us
  waiting for transfers between devices: 16.4 us -> 17.7 us
    pallas_call x5, Pallas kernels: 32.6 us -> 17.7 us  [the longest x1 5.82 us: body(): call(gram_kernel, pltpu.VMEM((32, 16, 128), F32), [pltpu.VMEM((3, 256, 40...]
    pallas_call x1, Pallas kernels: 33.4 us -> 20.1 us  [body(): call(solve_kernel, (shape(3, cells), shape(3, cells)), [pltpu.VMEM((25, 3...]
    all_to_all x1 -> x0, local copies, waits for them, and re-layouts: 1.75 us -> none  [body(): recv = lax.all_to_all(send, 'space', 0, 0, tiled=True)]
    all_to_all x1, waiting for transfers between devices: 6.72 us -> 8.03 us  [body(): recv = lax.all_to_all(send, 'space', 0, 0, tiled=True)]
    unnamed x8 -> x7, local copies, waits for them, and re-layouts: 2.71 us -> 2.16 us
  transfers between devices with their start and end apart: 3 -> 3, of which waited for: 2 -> 2; matrix products, arithmetic and copies ran while one was open for 1% -> 1% of each run, Pallas kernels for 14% -> 8%
where the time goes in v2:
time: 83.2 us; the launch traced here: 82.7 us
  Pallas kernels  37.9 us (46%)
  starting transfers between devices  24.2 us (29%)
  waiting for transfers between devices  17.7 us (21%)
  local copies, waits for them, and re-layouts  2.16 us (3%)
    pallas_call x1, Pallas kernels, body(): call(solve_kernel, (shape(3, cells), shape(3, cells)), [pltpu.VMEM((25, 3...  20.1 us
    all_to_all x1, starting transfers between devices, body(): recv = lax.all_to_all(send, 'space', 0, 0, tiled=True)  11.9 us
    all_to_all x1, waiting for transfers between devices, body(): recv_2 = lax.all_to_all(payload, 'space', 0, 0, tiled=True)  9.7 us
    all_to_all x1, starting transfers between devices, body(): recv_3 = lax.all_to_all(both, 'tm', 0, 0, tiled=True)  8.23 us
    all_to_all x1, waiting for transfers between devices, body(): recv = lax.all_to_all(send, 'space', 0, 0, tiled=True)  8.03 us
    pallas_call x1, Pallas kernels, body(): call(gram_kernel, pltpu.VMEM((32, 16, 128), F32), [pltpu.VMEM((3, 256, 40...  5.82 us
    pallas_call x1, Pallas kernels, body(): call(setup_kernel, (pltpu.VMEM((32, 32), F32), pltpu.VMEM((128, 128), F32...  4.84 us
    all_to_all x1, starting transfers between devices, body(): recv_2 = lax.all_to_all(payload, 'space', 0, 0, tiled=True)  4.13 us
  transfers between devices with their start and end apart: 3, of which 2 were waited for; matrix products, arithmetic and copies ran while one was open for 1% of the time, Pallas kernels for 8%

profile of v2, /device:TPU:1, one launch (start us, length us, event | category | flops | bytes accessed | tf_op | source)
XLA Modules:
  0.0 82.7 jit_solution(3540050238183766620)
XLA Ops:
  0.6 4.0 %buckets.1 = f32[32,1,1280]{2,1,0:T(1,128)} custom-call(s32[3,1,2048]{2,1,0:T(1,128)} %bitcast.11, s32[3,2048]{1,0:T(4,128)} %off_ref.1, f32[3,2048]{1,0:T(4,128)} %val_ref.1, f32[3,2048]{1,0:T(4,128)} %wgt_ref.1, bf16[64,8192]{1,0:T(8,128)(2,1)} %bitcast.6), custom_call_target="tpu_custom_call" | custom-call | tf_op jit(solution)/shard_map/buckets/pallas_call | solution.py:478
  4.6 11.9 %all-to-all-start = ((f32[32,1,1280]{2,1,0:T(1,128)}), f32[32,1,1280]{2,1,0:T(1,128)S(1)}, u32[]{:S(2)}, u32[]{:S(2)}) async-start(f32[32,1,1280]{2,1,0:T(1,128)} %buckets.1), calls=%async_computation | async-start | bytes 327680 | tf_op jit(solution)/shard_map/all_to_all | solution.py:484
  16.5 1.6 %field.1 = (f32[32,8192]{1,0:T(8,128)S(1)}, bf16[96,8192]{1,0:T(8,128)(2,1)S(1)}) custom-call(bf16[64,8192]{1,0:T(8,128)(2,1)} %bitcast.7, bf16[32,64]{1,0:T(8,128)(2,1)} %bitcast.9, f32[1,64]{1,0:T(1,128)} %bitcast.12), custom_call_target="tpu_custom_call" | custom-call | tf_op jit(solution)/shard_map/field/pallas_call | solution.py:485
  18.1 8.0 %all-to-all-done.recv_ref = f32[32,1,1280]{2,1,0:T(1,128)S(1)} async-done(((f32[32,1,1280]{2,1,0:T(1,128)}), f32[32,1,1280]{2,1,0:T(1,128)S(1)}, u32[]{:S(2)}, u32[]{:S(2)}) %all-to-all-start) | async-done | bytes 163872 | tf_op jit(solution)/shard_map/all_to_all | solution.py:484
  26.1 0.0 copy-start.2
  26.1 5.8 %grams.1 = f32[32,16,128]{2,1,0:T(8,128)} custom-call(f32[32,1,1280]{2,1,0:T(1,128)S(1)} %all-to-all-done.recv_ref, f32[32,8192]{1,0:T(8,128)S(1)} %get-tuple-element.8.ft_ref, bf16[96,8192]{1,0:T(8,128)(2,1)S(1)} %get-tuple-element.9.fp_ref), custom_call_target="tpu_custom_call" | custom-call | tf_op jit(solution)/shard_map/grams/pallas_call | solution.py:489
  31.9 4.1 %all-to-all-start.1 = ((f32[32,16,128]{2,1,0:T(8,128)}), f32[32,16,128]{2,1,0:T(8,128)S(1)}, u32[]{:S(2)}, u32[]{:S(2)}) async-start(f32[32,16,128]{2,1,0:T(8,128)} %grams.1), calls=%async_computation.1 | async-start | bytes 524288 | tf_op jit(solution)/shard_map/all_to_all | solution.py:501
  36.1 0.0 copy-done.2
  36.1 0.7 copy.11
  36.8 9.7 %all-to-all-done.1.recv_ref = f32[32,16,128]{2,1,0:T(8,128)S(1)} async-done(((f32[32,16,128]{2,1,0:T(8,128)}), f32[32,16,128]{2,1,0:T(8,128)S(1)}, u32[]{:S(2)}, u32[]{:S(2)}) %all-to-all-start.1) | async-done | bytes 262176 | tf_op jit(solution)/shard_map/all_to_all | solution.py:501
  46.5 1.5 %totals.1 = f32[8,24,128]{2,1,0:T(8,128)} custom-call(f32[32,16,128]{2,1,0:T(8,128)S(1)} %all-to-all-done.1.recv_ref, f32[3,32]{1,0:T(4,128)} %decay_ref.1, f32[32,3]{1,0:T(8,128)} %bitcast.8, f32[3]{0:T(128)} %infl_ref.1), custom_call_target="tpu_custom_call" | custom-call | tf_op jit(solution)/shard_map/totals/pallas_call | solution.py:503
  48.0 8.2 %all-to-all-start.2 = ((f32[8,24,128]{2,1,0:T(8,128)}), f32[8,24,128]{2,1,0:T(8,128)S(1)}, u32[]{:S(2)}, u32[]{:S(2)}) async-start(f32[8,24,128]{2,1,0:T(8,128)} %totals.1), calls=%async_computation.2 | async-start | bytes 196608 | tf_op jit(solution)/shard_map/all_to_all | solution.py:506
  56.2 4.8 %setup.1 = (f32[32,32]{1,0:T(8,128)S(1)}, f32[128,128]{1,0:T(8,128)S(1)}, f32[32,128]{1,0:T(8,128)S(1)}, bf16[96,8192]{1,0:T(8,128)(2,1)S(1)}) custom-call(f32[32,16,128]{2,1,0:T(8,128)S(1)} %all-to-all-done.1.recv_ref, bf16[32,64]{1,0:T(8,128)(2,1)} %bitcast.10, f32[1,64]{1,0:T(1,128)} %bitcast.13, bf16[96,8192]{1,0:T(8,128)(2,1)S(1)} %get-tuple-element.9.fp_ref), custom_call_target="tpu_custom_call" | custom-call | tf_op jit(solution)/shard_map/setup/pallas_call | solution.py:508
  61.1 0.0 copy-start
  61.1 0.6 copy-done
  61.7 0.0 all-to-all-done.2.recv_ref
  61.7 0.0 copy-start.1
  61.7 0.8 %copy-done.1 = f32[128,128]{1,0:T(8,128)S(1)} copy-done((f32[128,128]{1,0:T(8,128)S(1)}, f32[128,128]{1,0:T(8,128)}, u32[]{:S(2)}) %copy-start.1) | copy-done | bytes 65560
  62.5 20.1 %solve.1 = (f32[3,8192]{1,0:T(4,128)}, f32[3,8192]{1,0:T(4,128)}) custom-call(s32[1]{0:T(128)} %bitcast.pos_ref, f32[8,24,128]{2,1,0:T(8,128)S(1)} %all-to-all-done.2.recv_ref, f32[32,32]{1,0:T(8,128)S(1)} %get-tuple-element.10.linv_ref, f32[128,128]{1,0:T(8,128)S(1)} %copy-done.1, f32[32,128]{1,0:T(8,128)S(1)} %get-tuple-element.12.k3_ref, ...), custom_call_target="tpu_custom_call" | custom-call | tf_op jit(solution)/shard_map/solve/pallas_call | solution.py:520
Async XLA Ops:
  4.6 21.5 %all-to-all-start = ((f32[32,1,1280]{2,1,0:T(1,128)}), f32[32,1,1280]{2,1,0:T(1,128)S(1)}, u32[]{:S(2)}, u32[]{:S(2)}) async-start(f32[32,1,1280]{2,1,0:T(1,128)} %buckets.1), calls=%async_computation | async-start | bytes 327680 | tf_op jit(solution)/shard_map/all_to_all | solution.py:484
  26.1 10.0 %copy-start.2 = (f32[3,32]{1,0:T(4,128)S(1)}, f32[3,32]{1,0:T(4,128)}, u32[]{:S(2)}) copy-start(f32[3,32]{1,0:T(4,128)} %decay_ref.1) | copy-start | bytes 1156
  31.9 14.5 %all-to-all-start.1 = ((f32[32,16,128]{2,1,0:T(8,128)}), f32[32,16,128]{2,1,0:T(8,128)S(1)}, u32[]{:S(2)}, u32[]{:S(2)}) async-start(f32[32,16,128]{2,1,0:T(8,128)} %grams.1), calls=%async_computation.1 | async-start | bytes 524288 | tf_op jit(solution)/shard_map/all_to_all | solution.py:501
  48.0 13.7 %all-to-all-start.2 = ((f32[8,24,128]{2,1,0:T(8,128)}), f32[8,24,128]{2,1,0:T(8,128)S(1)}, u32[]{:S(2)}, u32[]{:S(2)}) async-start(f32[8,24,128]{2,1,0:T(8,128)} %totals.1), calls=%async_computation.2 | async-start | bytes 196608 | tf_op jit(solution)/shard_map/all_to_all | solution.py:506
  61.1 0.6 copy-start
  61.7 0.8 %copy-start.1 = (f32[128,128]{1,0:T(8,128)S(1)}, f32[128,128]{1,0:T(8,128)}, u32[]{:S(2)}) copy-start(f32[128,128]{1,0:T(8,128)} %copy-done) | copy-start | bytes 196612

commit v3 on v2

--- a/solution.py
+++ b/solution.py
@@ -31,26 +31,53 @@
     return top, x - top
 
 
-def bucket_kernel(owner_ref, off_ref, val_ref, wgt_ref, bt_ref, send_ref, lhs_s, rt_s):
+def thirds(x):
+    parts = []
+    for _ in range(3):
+        parts.append(x.astype(BF16))
+        x = x - parts[-1].astype(F32)
+    return parts
+
+
+def packed(line, rows):
+    line = jnp.broadcast_to(line, (16, LANES)).astype(BF16)
+    return jnp.concatenate([line] * (rows // 16), axis=0)
+
+
+def counter16(rows):
+    return iota((rows, LANES), 0).astype(F32).astype(BF16)
+
+
+def bucket_kernel(owner_ref, off_ref, val_ref, wgt_ref, bt_hbm, send_ref, bt_ref, oh_s, lhs_s, rt_s, sem):
+    fetch = pltpu.make_async_copy(bt_hbm, bt_ref, sem)
+    fetch.start()
     days, _, obs = owner_ref.shape
     owners = send_ref.shape[0]
     chunks = obs // LANES
     upper = (iota((LANES, LANES), 0) < iota((LANES, LANES), 1)).astype(F32)
     counter = jnp.concatenate([upper, jnp.ones((LANES, LANES), F32)], axis=1).astype(BF16)
-    sub_owner = iota((owners, LANES), 0)
-    sub_slot = iota((LANES, LANES), 0)
+    sub_owner = counter16(owners)
+    sub_slot = counter16(LANES)
+    one, zero = jnp.ones((), BF16), jnp.zeros((), BF16)
+    for d in range(days):
+        for c in range(chunks):
+            at = slice(c * LANES, (c + 1) * LANES)
+            k = (d * chunks + c) * owners
+            hit = sub_owner == packed(owner_ref[d, :, at].astype(F32), owners)
+            oh_s[k : k + owners] = jnp.where(hit, one, zero)
+    counts = jnp.dot(oh_s[...], counter, preferred_element_type=F32)
     for d in range(days):
         base = jnp.zeros((owners, LANES), F32)
         for c in range(chunks):
             at = slice(c * LANES, (c + 1) * LANES)
-            hit = sub_owner == owner_ref[d, :, at]
-            one_hot = jnp.where(hit, 1.0, 0.0)
-            counts = lax.dot_general(
-                one_hot.astype(BF16), counter, (((1,), (0,)), ((), ())), preferred_element_type=F32
+            k = (d * chunks + c) * owners
+            one_hot = oh_s[k : k + owners]
+            count = counts[k : k + owners]
+            slot = jnp.sum(
+                one_hot.astype(F32) * (count[:, :LANES] + base), axis=0, keepdims=True
             )
-            slot = jnp.sum(one_hot * (counts[:, :LANES] + base), axis=0, keepdims=True)
-            base = base + counts[:, LANES:]
-            rt_s[d, :, at] = jnp.where(sub_slot == slot.astype(I32), 1.0, 0.0).astype(BF16)
+            base = base + count[:, LANES:]
+            rt_s[d, :, at] = jnp.where(sub_slot == packed(slot, LANES), one, zero)
             weight = wgt_ref[d : d + 1, at]
             offset = off_ref[d : d + 1, at]
             fields = (
@@ -60,13 +87,13 @@
                 (offset & 127).astype(F32),
             )
             for f, row in enumerate(fields):
-                lhs_s[d, f * owners : (f + 1) * owners, at] = jnp.where(hit, row, 0.0).astype(BF16)
-    for d in range(days):
+                lhs_s[d, f * owners : (f + 1) * owners, at] = one_hot * packed(row, owners)
         got = nt(lhs_s[d], rt_s[d])
         part = [got[f * owners : (f + 1) * owners] for f in range(6)]
         for f, x in enumerate((part[0] + part[1], part[2] + part[3], part[4] * 128.0 + part[5])):
             j = f * days + d
             send_ref[:, 0, j * LANES : (j + 1) * LANES] = x
+    fetch.wait()
     gram = nt(bt_ref[...], bt_ref[...])
     send_ref[:, 0, 9 * LANES : 10 * LANES] = jnp.concatenate([gram[:32], gram[32:]], axis=1)
 
@@ -86,13 +113,8 @@
 def gram_kernel(recv_ref, ft_ref, fp_ref, out_ref, lhs_s, rhs_s, wc_s, uc_s, pay_s):
     readers = recv_ref.shape[0]
     days = 3
-    sub64 = iota((64, LANES), 0).astype(F32).astype(BF16)
-    sub128 = iota((LANES, LANES), 0).astype(F32).astype(BF16)
-    zero = jnp.zeros((), BF16)
-
-    def packed(x, r, rows):
-        line = jnp.broadcast_to(x[r : r + 1], (16, LANES)).astype(BF16)
-        return jnp.concatenate([line] * (rows // 16), axis=0)
+    sub64, sub128 = counter16(64), counter16(LANES)
+    one, zero = jnp.ones((), BF16), jnp.zeros((), BF16)
 
     for d in range(days):
         w = halves(recv_ref[:, 0, d * LANES : (d + 1) * LANES])
@@ -101,10 +123,10 @@
         high, low = (offset >> 7).astype(F32), (offset & 127).astype(F32)
         for r in range(readers):
             at = slice(r * LANES, (r + 1) * LANES)
-            hit = sub64 == packed(high, r, 64)
+            hit = sub64 == packed(high[r : r + 1], 64)
             for f, x in enumerate(w + u):
-                lhs_s[d, f * 64 : (f + 1) * 64, at] = jnp.where(hit, packed(x, r, 64), zero)
-            rhs_s[d, :, at] = jnp.where(sub128 == packed(low, r, LANES), jnp.ones((), BF16), zero)
+                lhs_s[d, f * 64 : (f + 1) * 64, at] = jnp.where(hit, packed(x[r : r + 1], 64), zero)
+            rhs_s[d, :, at] = jnp.where(sub128 == packed(low[r : r + 1], LANES), one, zero)
         got = nt(lhs_s[d], rhs_s[d])
         wc_s[d] = got[:64] + got[64:128]
         uc_s[d] = got[128:192] + got[192:]
@@ -187,7 +209,8 @@
         q, s = divmod(k, 8)
         for n, a in enumerate(tiles):
             r = [wide(a[q][s + i : s + i + 1, :]) for i in range(4)]
-            m = {(i, j): wide(r[i][:, k + j : k + j + 1]) for i in range(4) for j in range(i, 4)}
+            cq = [jnp.maximum(wide(a[q][:, k + i : k + i + 1]), -jnp.inf) for i in range(4)]
+            m = {(i, j): wide(cq[j][s + i : s + i + 1, :]) for i in range(4) for j in range(i, 4)}
             ia = 1.0 / (m[0, 0] * m[1, 1] - m[0, 1] * m[0, 1])
             x02 = (m[1, 1] * m[0, 2] - m[0, 1] * m[1, 2]) * ia
             x03 = (m[1, 1] * m[0, 3] - m[0, 1] * m[1, 3]) * ia
@@ -213,7 +236,7 @@
             for t in range(q, 4):
                 if t == q and s == 4:
                     continue
-                c = [wide(a[t][:, k + i : k + i + 1]) for i in range(4)]
+                c = cq if t == q else [wide(a[t][:, k + i : k + i + 1]) for i in range(4)]
                 delta = (c[0] * v0 + c[1] * v1) + (c[2] * v2 + c[3] * v3)
                 if t == q:
                     delta = jnp.where(low, delta, 0.0)
@@ -249,7 +272,7 @@
     return nn_high(jnp.transpose(a), b)
 
 
-def setup_kernel(recv_ref, probe_ref, scale_ref, fp_ref, linv_ref, bd_ref, k3_ref, b_ref):
+def setup_kernel(recv_ref, probe_ref, scale_ref, fp_ref, b_ref):
     lane = iota((32, LANES), 1)
     gram = jnp.zeros((32, LANES), F32)
     for i in range(16):
@@ -278,17 +301,10 @@
     (u,), (v,) = eliminate([jnp.concatenate([prior, eye, zero64], axis=1)])
     prec = tn_high(v[:, 32:64], u[:, 32:64])
     prec = 0.5 * (prec + jnp.transpose(prec))
-    linv_ref[...] = linv
-    k3_ref[...] = jnp.concatenate([prec, prec, prec, jnp.zeros((32, 32), F32)], axis=1)
-    lt = jnp.transpose(linv)
-    zero32 = jnp.zeros((32, 32), F32)
-    bd_ref[...] = jnp.concatenate(
-        [
-            jnp.concatenate([x if i == j else zero32 for j in range(4)], axis=1)
-            for i, x in enumerate((lt, lt, lt, eye))
-        ],
-        axis=0,
-    )
+    cells = fp_ref.shape[1]
+    zero64 = jnp.zeros((32, 64), F32)
+    for k, part in enumerate(thirds(jnp.concatenate([linv, prec, zero64], axis=1))):
+        b_ref[32 * k : 32 * k + 32, cells:] = part
     one, two = halves(linv)
     basis = lax.dot_general(
         jnp.concatenate([one, one, two], axis=1).astype(BF16),
@@ -297,14 +313,28 @@
         preferred_element_type=F32,
     )
     top = basis.astype(BF16)
-    b_ref[0:32] = top
-    b_ref[32:64] = (basis - top.astype(F32)).astype(BF16)
-    b_ref[64:96] = top
-
-
-def solve_kernel(pos_ref, recv_ref, linv_ref, bd_ref, k3_ref, b_ref, mean_ref, spread_ref, e_s, x_s):
+    b_ref[0:32, :cells] = top
+    b_ref[32:64, :cells] = (basis - top.astype(F32)).astype(BF16)
+    b_ref[64:96, :cells] = top
+
+
+def solve_kernel(pos_ref, recv_ref, b_ref, mean_ref, spread_ref, e_s, x_s):
     lane = iota((32, LANES), 1)
-    k3 = k3_ref[...]
+    cells = b_ref.shape[1] - LANES
+    small = b_ref[0:32, cells:].astype(F32) + b_ref[32:64, cells:].astype(F32)
+    small = small + b_ref[64:96, cells:].astype(F32)
+    linv, prec = small[:, :32], small[:, 32:64]
+    lt = jnp.transpose(linv)
+    zero32 = jnp.zeros((32, 32), F32)
+    eye = (iota((32, 32), 0) == iota((32, 32), 1)).astype(F32)
+    k3 = jnp.concatenate([prec, prec, prec, zero32], axis=1)
+    per_day = jnp.concatenate(
+        [
+            jnp.concatenate([x if i == j else zero32 for j in range(4)], axis=1)
+            for i, x in enumerate((lt, lt, lt, eye))
+        ],
+        axis=0,
+    )
     r16, c16 = iota((16, 16), 0), iota((16, 16), 1)
     zero_row = jnp.zeros((1, LANES), F32)
     dcols = []
@@ -336,9 +366,9 @@
         x_s[:, r * LANES : (r + 1) * LANES] = jnp.concatenate(
             slabs + gs + [jnp.zeros((32, 29), F32)], axis=1
         )
-    z = nn_high(linv_ref[...], x_s[...])
+    z = nn_high(linv, x_s[...])
     zs = jnp.concatenate([z[:, r * LANES : (r + 1) * LANES] for r in range(8)], axis=0)
-    hs = nn_high(zs, bd_ref[...])
+    hs = nn_high(zs, per_day)
     first = [recv_ref[b // 3, 16 + b % 3 : 17 + b % 3, :] for b in range(24)]
     first.append(jnp.where(iota((1, LANES), 1) < 32, 1.0, 0.0))
     second = [recv_ref[b // 3, 19 + b % 3 : 20 + b % 3, :] for b in range(24)] + [zero_row]
@@ -432,20 +462,16 @@
     lhs = jnp.concatenate(rows + sums + [jnp.zeros((5, 32), F32)], axis=0)
     one, two = halves(lhs)
     lhs = jnp.concatenate([one, one, two], axis=1).astype(BF16)
-    cells = b_ref.shape[1]
-    step = 512
-
-    def finish(c, _):
-        at = pl.ds(pl.multiple_of(c * step, step), step)
-        b = b_ref[:, at]
+    step = 1024
+    for c in range(0, cells, step):
+        b = b_ref[:, c : c + step]
         y = lax.dot_general(lhs, b, (((1,), (0,)), ((), ())), preferred_element_type=F32)
         wide = b[0:32].astype(F32) + b[32:64].astype(F32)
         for d in range(3):
-            spread_ref[d : d + 1, at] = jnp.sum(y[32 * d : 32 * d + 32] * wide, axis=0, keepdims=True)
-            mean_ref[d : d + 1, at] = y[96 + d : 97 + d]
-        return 0
-
-    lax.fori_loop(0, cells // step, finish, 0, unroll=2)
+            spread_ref[d : d + 1, c : c + step] = jnp.sum(
+                y[32 * d : 32 * d + 32] * wide, axis=0, keepdims=True
+            )
+        mean_ref[:, c : c + step] = y[96:99]
 
 
 def shape(*dims, dtype=F32):
@@ -478,7 +504,14 @@
     send = call(
         bucket_kernel,
         pltpu.VMEM((32, 1, 1280), F32),
-        [pltpu.VMEM((3, 192, 2048), BF16), pltpu.VMEM((3, 128, 2048), BF16)],
+        [
+            pltpu.VMEM(bt.shape, BF16),
+            pltpu.VMEM((3 * 16 * 32, 128), BF16),
+            pltpu.VMEM((3, 192, 2048), BF16),
+            pltpu.VMEM((3, 128, 2048), BF16),
+            pltpu.SemaphoreType.DMA,
+        ],
+        in_specs=[VM, VM, VM, VM, pl.BlockSpec(memory_space=pl.ANY)],
         name="buckets",
     )(owner, obs_offset, obs_value, obs_weight, bt)
     recv = lax.all_to_all(send, "space", 0, 0, tiled=True)
@@ -505,25 +538,20 @@
     )
     recv_3 = lax.all_to_all(both, "tm", 0, 0, tiled=True)
     (recv_3,) = on_chip(recv_3)
-    linv, bd, k3, basis = call(
+    basis = call(
         setup_kernel,
-        (
-            pltpu.VMEM((32, 32), F32),
-            pltpu.VMEM((128, 128), F32),
-            pltpu.VMEM((32, 128), F32),
-            pltpu.VMEM((96, cells), BF16),
-        ),
+        pltpu.VMEM((96, cells + 128), BF16),
         name="setup",
     )(recv_2, probe_t, scale, fp)
-    linv, bd, k3, basis = on_chip(linv, bd, k3, basis)
+    (basis,) = on_chip(basis)
     pos = lax.axis_index("tm").astype(I32).reshape(1)
     mean, spread = call(
         solve_kernel,
         (shape(3, cells), shape(3, cells)),
         [pltpu.VMEM((25, 32, 128), F32), pltpu.VMEM((32, 1024), F32)],
-        in_specs=[SM, VM, VM, VM, VM, VM],
+        in_specs=[SM, VM, VM],
         name="solve",
-    )(pos, recv_3, linv, bd, k3, basis)
+    )(pos, recv_3, basis)
     return mean, spread
 
 

time: 83.2 us -> 77.8 us (0.935)
  Pallas kernels: 37.9 us -> 33.1 us
  local copies, waits for them, and re-layouts: 2.16 us -> 0.7 us
    pallas_call x1, Pallas kernels: 20.1 us -> 16 us  [body(): call(solve_kernel, (shape(3, cells), shape(3, cells)), [pltpu.VMEM((25, 3...]
    unnamed x7 -> x3, local copies, waits for them, and re-layouts: 2.16 us -> 0.7 us
  transfers between devices with their start and end apart: 3 -> 3, of which waited for: 2 -> 3; matrix products, arithmetic and copies ran while one was open for 1% -> 1% of each run, Pallas kernels for 8% -> 7%
where the time goes in v3:
time: 77.8 us; the launch traced here: 77.3 us
  Pallas kernels  33.1 us (43%)
  starting transfers between devices  24.2 us (31%)
  waiting for transfers between devices  18.5 us (24%)
    pallas_call x1, Pallas kernels, body(): call(solve_kernel, (shape(3, cells), shape(3, cells)), [pltpu.VMEM((25, 3...  16 us
    all_to_all x1, starting transfers between devices, body(): recv = lax.all_to_all(send, 'space', 0, 0, tiled=True)  11.9 us
    all_to_all x1, waiting for transfers between devices, body(): recv_2 = lax.all_to_all(payload, 'space', 0, 0, tiled=True)  9.7 us
    all_to_all x1, starting transfers between devices, body(): recv_3 = lax.all_to_all(both, 'tm', 0, 0, tiled=True)  8.23 us
    all_to_all x1, waiting for transfers between devices, body(): recv = lax.all_to_all(send, 'space', 0, 0, tiled=True)  8.04 us
    pallas_call x1, Pallas kernels, body(): call(gram_kernel, pltpu.VMEM((32, 16, 128), F32), [pltpu.VMEM((3, 256, 40...  5.82 us
    pallas_call x1, Pallas kernels, body(): call(setup_kernel, pltpu.VMEM((96, cells + 128), BF16), name='setup')  4.17 us
    all_to_all x1, starting transfers between devices, body(): recv_2 = lax.all_to_all(payload, 'space', 0, 0, tiled=True)  4.13 us
  transfers between devices with their start and end apart: 3, of which 3 were waited for; matrix products, arithmetic and copies ran while one was open for 1% of the time, Pallas kernels for 7%

profile of v3, /device:TPU:1, one launch (start us, length us, event | category | flops | bytes accessed | tf_op | source)
XLA Modules:
  0.0 77.3 jit_solution(11224433410750796887)
XLA Ops:
  0.6 4.0 %buckets.1 = f32[32,1,1280]{2,1,0:T(1,128)} custom-call(s32[3,1,2048]{2,1,0:T(1,128)} %bitcast.11, s32[3,2048]{1,0:T(4,128)} %off_ref.1, f32[3,2048]{1,0:T(4,128)} %val_ref.1, f32[3,2048]{1,0:T(4,128)} %wgt_ref.1, bf16[64,8192]{1,0:T(8,128)(2,1)} %bitcast.6), custom_call_target="tpu_custom_call" | custom-call | tf_op jit(solution)/shard_map/buckets/pallas_call | solution.py:504
  4.7 11.9 %all-to-all-start = ((f32[32,1,1280]{2,1,0:T(1,128)}), f32[32,1,1280]{2,1,0:T(1,128)S(1)}, u32[]{:S(2)}, u32[]{:S(2)}) async-start(f32[32,1,1280]{2,1,0:T(1,128)} %buckets.1), calls=%async_computation | async-start | bytes 327680 | tf_op jit(solution)/shard_map/all_to_all | solution.py:517
  16.5 1.6 %field.1 = (f32[32,8192]{1,0:T(8,128)S(1)}, bf16[96,8192]{1,0:T(8,128)(2,1)S(1)}) custom-call(bf16[64,8192]{1,0:T(8,128)(2,1)} %bitcast.7, bf16[32,64]{1,0:T(8,128)(2,1)} %bitcast.9, f32[1,64]{1,0:T(1,128)} %bitcast.12), custom_call_target="tpu_custom_call" | custom-call | tf_op jit(solution)/shard_map/field/pallas_call | solution.py:518
  18.1 8.0 %all-to-all-done.recv_ref = f32[32,1,1280]{2,1,0:T(1,128)S(1)} async-done(((f32[32,1,1280]{2,1,0:T(1,128)}), f32[32,1,1280]{2,1,0:T(1,128)S(1)}, u32[]{:S(2)}, u32[]{:S(2)}) %all-to-all-start) | async-done | bytes 163872 | tf_op jit(solution)/shard_map/all_to_all | solution.py:517
  26.2 0.0 copy-start
  26.2 5.8 %grams.1 = f32[32,16,128]{2,1,0:T(8,128)} custom-call(f32[32,1,1280]{2,1,0:T(1,128)S(1)} %all-to-all-done.recv_ref, f32[32,8192]{1,0:T(8,128)S(1)} %get-tuple-element.4.ft_ref, bf16[96,8192]{1,0:T(8,128)(2,1)S(1)} %get-tuple-element.5.fp_ref), custom_call_target="tpu_custom_call" | custom-call | tf_op jit(solution)/shard_map/grams/pallas_call | solution.py:522
  32.0 4.1 %all-to-all-start.1 = ((f32[32,16,128]{2,1,0:T(8,128)}), f32[32,16,128]{2,1,0:T(8,128)S(1)}, u32[]{:S(2)}, u32[]{:S(2)}) async-start(f32[32,16,128]{2,1,0:T(8,128)} %grams.1), calls=%async_computation.1 | async-start | bytes 524288 | tf_op jit(solution)/shard_map/all_to_all | solution.py:534
  36.1 0.0 copy-done
  36.1 0.7 copy.11
  36.8 9.7 %all-to-all-done.1.recv_ref = f32[32,16,128]{2,1,0:T(8,128)S(1)} async-done(((f32[32,16,128]{2,1,0:T(8,128)}), f32[32,16,128]{2,1,0:T(8,128)S(1)}, u32[]{:S(2)}, u32[]{:S(2)}) %all-to-all-start.1) | async-done | bytes 262176 | tf_op jit(solution)/shard_map/all_to_all | solution.py:534
  46.5 1.5 %totals.1 = f32[8,24,128]{2,1,0:T(8,128)} custom-call(f32[32,16,128]{2,1,0:T(8,128)S(1)} %all-to-all-done.1.recv_ref, f32[3,32]{1,0:T(4,128)} %decay_ref.1, f32[32,3]{1,0:T(8,128)} %bitcast.8, f32[3]{0:T(128)} %infl_ref.1), custom_call_target="tpu_custom_call" | custom-call | tf_op jit(solution)/shard_map/totals/pallas_call | solution.py:536
  48.0 8.2 %all-to-all-start.2 = ((f32[8,24,128]{2,1,0:T(8,128)}), f32[8,24,128]{2,1,0:T(8,128)S(1)}, u32[]{:S(2)}, u32[]{:S(2)}) async-start(f32[8,24,128]{2,1,0:T(8,128)} %totals.1), calls=%async_computation.2 | async-start | bytes 196608 | tf_op jit(solution)/shard_map/all_to_all | solution.py:539
  56.3 4.2 %setup.1.b_ref = bf16[96,8320]{1,0:T(8,128)(2,1)S(1)} custom-call(f32[32,16,128]{2,1,0:T(8,128)S(1)} %all-to-all-done.1.recv_ref, bf16[32,64]{1,0:T(8,128)(2,1)} %bitcast.10, f32[1,64]{1,0:T(1,128)} %bitcast.13, bf16[96,8192]{1,0:T(8,128)(2,1)S(1)} %get-tuple-element.5.fp_ref), custom_call_target="tpu_custom_call" | custom-call | tf_op jit(solution)/shard_map/setup/pallas_call | solution.py:541
  60.5 0.8 %all-to-all-done.2.recv_ref = f32[8,24,128]{2,1,0:T(8,128)S(1)} async-done(((f32[8,24,128]{2,1,0:T(8,128)}), f32[8,24,128]{2,1,0:T(8,128)S(1)}, u32[]{:S(2)}, u32[]{:S(2)}) %all-to-all-start.2) | async-done | bytes 98336 | tf_op jit(solution)/shard_map/all_to_all | solution.py:539
  61.3 16.0 %solve.1 = (f32[3,8192]{1,0:T(4,128)}, f32[3,8192]{1,0:T(4,128)}) custom-call(s32[1]{0:T(128)} %bitcast.pos_ref, f32[8,24,128]{2,1,0:T(8,128)S(1)} %all-to-all-done.2.recv_ref, bf16[96,8320]{1,0:T(8,128)(2,1)S(1)} %setup.1.b_ref), custom_call_target="tpu_custom_call" | custom-call | tf_op jit(solution)/shard_map/solve/pallas_call | solution.py:548
Async XLA Ops:
  4.7 21.5 %all-to-all-start = ((f32[32,1,1280]{2,1,0:T(1,128)}), f32[32,1,1280]{2,1,0:T(1,128)S(1)}, u32[]{:S(2)}, u32[]{:S(2)}) async-start(f32[32,1,1280]{2,1,0:T(1,128)} %buckets.1), calls=%async_computation | async-start | bytes 327680 | tf_op jit(solution)/shard_map/all_to_all | solution.py:517
  26.2 10.0 %copy-start = (f32[3,32]{1,0:T(4,128)S(1)}, f32[3,32]{1,0:T(4,128)}, u32[]{:S(2)}) copy-start(f32[3,32]{1,0:T(4,128)} %decay_ref.1) | copy-start | bytes 1156
  32.0 14.5 %all-to-all-start.1 = ((f32[32,16,128]{2,1,0:T(8,128)}), f32[32,16,128]{2,1,0:T(8,128)S(1)}, u32[]{:S(2)}, u32[]{:S(2)}) async-start(f32[32,16,128]{2,1,0:T(8,128)} %grams.1), calls=%async_computation.1 | async-start | bytes 524288 | tf_op jit(solution)/shard_map/all_to_all | solution.py:534
  48.0 13.2 %all-to-all-start.2 = ((f32[8,24,128]{2,1,0:T(8,128)}), f32[8,24,128]{2,1,0:T(8,128)S(1)}, u32[]{:S(2)}, u32[]{:S(2)}) async-start(f32[8,24,128]{2,1,0:T(8,128)} %totals.1), calls=%async_computation.2 | async-start | bytes 196608 | tf_op jit(solution)/shard_map/all_to_all | solution.py:539

commit v4 on v3

--- a/solution.py
+++ b/solution.py
@@ -98,16 +98,32 @@
     send_ref[:, 0, 9 * LANES : 10 * LANES] = jnp.concatenate([gram[:32], gram[32:]], axis=1)
 
 
-def field_kernel(bt_ref, probe_ref, scale_ref, ft_ref, fp_ref):
-    scaled = (probe_ref[...].astype(F32) * scale_ref[...]).astype(BF16)
-    ft = lax.dot_general(
-        scaled, bt_ref[...], (((1,), (0,)), ((), ())), preferred_element_type=F32
-    )
+def field_kernel(
+    bt_ref, probe_ref, scale_ref, decay_ref, decay_t_ref, infl_ref, ft_ref, fp_ref, probe_out, days_ref
+):
+    scale = scale_ref[...]
+    scaled = (probe_ref[...].astype(F32) * scale).astype(BF16)
+    ft = jnp.dot(scaled, bt_ref[...], preferred_element_type=F32)
     ft_ref[...] = ft
     top = ft.astype(BF16)
     fp_ref[0:32] = top
     fp_ref[32:64] = (ft - top.astype(F32)).astype(BF16)
     fp_ref[64:96] = top
+    probe_out[0:32] = scaled.astype(F32)
+    probe_out[32:40] = jnp.broadcast_to(scale * scale, (8, scale.shape[1]))
+    lane16, lane1 = iota((16, LANES), 1), iota((1, LANES), 1)
+    columns = jnp.zeros((16, LANES), F32)
+    first, second = [], []
+    for d in range(3):
+        columns = jnp.where(lane16 == 105 + 2 * d, decay_t_ref[:16, d : d + 1], columns)
+        columns = jnp.where(lane16 == 106 + 2 * d, decay_t_ref[16:, d : d + 1], columns)
+        gamma = 1.0 / infl_ref[d]
+        decay = jnp.concatenate([decay_ref[d : d + 1, :]] * 4, axis=1)
+        right = (lane1 >= 64) & (lane1 < 96)
+        first.append(jnp.where(lane1 < 32, gamma, jnp.where(lane1 < 64, -gamma * decay, 0.0)))
+        second.append(jnp.where(lane1 < 32, gamma * decay, jnp.where(right, -gamma, 0.0)))
+    rows = first + second + [jnp.zeros((2, LANES), F32)]
+    days_ref[...] = jnp.concatenate([columns] + rows, axis=0)
 
 
 def gram_kernel(recv_ref, ft_ref, fp_ref, out_ref, lhs_s, rhs_s, wc_s, uc_s, pay_s):
@@ -171,30 +187,9 @@
         out_ref[r] = pay
 
 
-def total_kernel(recv_ref, decay_ref, decay_t_ref, infl_ref, out_ref):
+def total_kernel(recv_ref, days_ref, out_ref):
     total = jnp.sum(recv_ref[...], axis=0)
-    lane16 = iota((16, LANES), 1)
-    lane1 = iota((1, LANES), 1)
-    rows = []
-    for d in range(3):
-        total = jnp.where(lane16 == 105 + 2 * d, decay_t_ref[:16, d : d + 1], total)
-        total = jnp.where(lane16 == 106 + 2 * d, decay_t_ref[16:, d : d + 1], total)
-    for d in range(3):
-        gamma = 1.0 / infl_ref[d]
-        dec = decay_ref[d : d + 1, :]
-        dec128 = jnp.concatenate([dec, dec, dec, dec], axis=1)
-        rows.append(jnp.where(lane1 < 32, gamma, jnp.where(lane1 < 64, -gamma * dec128, 0.0)))
-    for d in range(3):
-        gamma = 1.0 / infl_ref[d]
-        dec = decay_ref[d : d + 1, :]
-        dec128 = jnp.concatenate([dec, dec, dec, dec], axis=1)
-        rows.append(
-            jnp.where(
-                lane1 < 32, gamma * dec128, jnp.where((lane1 >= 64) & (lane1 < 96), -gamma, 0.0)
-            )
-        )
-    rows.append(jnp.zeros((2, LANES), F32))
-    both = jnp.concatenate([total] + rows, axis=0)
+    both = days_ref[...] + jnp.concatenate([total, jnp.zeros((8, LANES), F32)], axis=0)
     for r in range(out_ref.shape[0]):
         out_ref[r] = both
 
@@ -272,7 +267,7 @@
     return nn_high(jnp.transpose(a), b)
 
 
-def setup_kernel(recv_ref, probe_ref, scale_ref, fp_ref, b_ref):
+def setup_kernel(recv_ref, probe_ref, small_ref):
     lane = iota((32, LANES), 1)
     gram = jnp.zeros((32, LANES), F32)
     for i in range(16):
@@ -280,8 +275,7 @@
         moved = pltpu.roll(slab, (8 * i - 112) % LANES, 1)
         gram = jnp.where((lane >> 3) == i, moved, gram)
     gram = jnp.concatenate([gram[:, :64], gram[:, 64:]], axis=0)
-    scale = scale_ref[...]
-    scaled = (probe_ref[...].astype(F32) * scale).astype(BF16).astype(F32)
+    scaled = probe_ref[0:32]
     half = nn_high(scaled, gram)
     core = lax.dot_general(
         half, scaled, (((1,), (1,)), ((), ())), precision=HIGHEST, preferred_element_type=F32
@@ -292,7 +286,7 @@
     linv = finish_factor(u)[:, 32:64]
     projected = nn_high(linv, half)
     prior = lax.dot_general(
-        projected * (scale * scale),
+        projected * probe_ref[32:33],
         projected,
         (((1,), (1,)), ((), ())),
         precision=HIGHEST,
@@ -301,29 +295,22 @@
     (u,), (v,) = eliminate([jnp.concatenate([prior, eye, zero64], axis=1)])
     prec = tn_high(v[:, 32:64], u[:, 32:64])
     prec = 0.5 * (prec + jnp.transpose(prec))
+    small_ref[...] = jnp.concatenate([linv, prec, zero64], axis=1)
+
+
+def solve_kernel(recv_ref, small_ref, fp_ref, mean_hbm, spread_hbm, e_s, x_s, b_s, mean_ref, spread_ref, sems):
+    lane = iota((32, LANES), 1)
+    linv, prec = small_ref[:, :32], small_ref[:, 32:64]
     cells = fp_ref.shape[1]
-    zero64 = jnp.zeros((32, 64), F32)
-    for k, part in enumerate(thirds(jnp.concatenate([linv, prec, zero64], axis=1))):
-        b_ref[32 * k : 32 * k + 32, cells:] = part
+    step = 1024
     one, two = halves(linv)
-    basis = lax.dot_general(
-        jnp.concatenate([one, one, two], axis=1).astype(BF16),
-        fp_ref[...],
-        (((1,), (0,)), ((), ())),
-        preferred_element_type=F32,
-    )
-    top = basis.astype(BF16)
-    b_ref[0:32, :cells] = top
-    b_ref[32:64, :cells] = (basis - top.astype(F32)).astype(BF16)
-    b_ref[64:96, :cells] = top
-
-
-def solve_kernel(pos_ref, recv_ref, b_ref, mean_ref, spread_ref, e_s, x_s):
-    lane = iota((32, LANES), 1)
-    cells = b_ref.shape[1] - LANES
-    small = b_ref[0:32, cells:].astype(F32) + b_ref[32:64, cells:].astype(F32)
-    small = small + b_ref[64:96, cells:].astype(F32)
-    linv, prec = small[:, :32], small[:, 32:64]
+    onto = jnp.concatenate([one, one, two], axis=1).astype(BF16)
+    for c in range(0, cells, step):
+        basis = jnp.dot(onto, fp_ref[:, c : c + step], preferred_element_type=F32)
+        top = basis.astype(BF16)
+        b_s[0:32, c : c + step] = top
+        b_s[32:64, c : c + step] = (basis - top.astype(F32)).astype(BF16)
+        b_s[64:96, c : c + step] = top
     lt = jnp.transpose(linv)
     zero32 = jnp.zeros((32, 32), F32)
     eye = (iota((32, 32), 0) == iota((32, 32), 1)).astype(F32)
@@ -383,7 +370,7 @@
             vec = h if d == 0 else pltpu.roll(h, LANES - d, 1)
             e = e + jnp.where(lane < 32, mat, jnp.where(lane == 96, vec, 0.0))
         e_s[b] = e
-    start = 3 * pos_ref[0]
+    start = 3 * lax.axis_index("tm")
     nodes = [e_s[lax.rem(start + j, 25)] for j in range(25)]
 
     plan = [
@@ -462,16 +449,23 @@
     lhs = jnp.concatenate(rows + sums + [jnp.zeros((5, 32), F32)], axis=0)
     one, two = halves(lhs)
     lhs = jnp.concatenate([one, one, two], axis=1).astype(BF16)
-    step = 1024
-    for c in range(0, cells, step):
-        b = b_ref[:, c : c + step]
-        y = lax.dot_general(lhs, b, (((1,), (0,)), ((), ())), preferred_element_type=F32)
-        wide = b[0:32].astype(F32) + b[32:64].astype(F32)
-        for d in range(3):
-            spread_ref[d : d + 1, c : c + step] = jnp.sum(
-                y[32 * d : 32 * d + 32] * wide, axis=0, keepdims=True
-            )
-        mean_ref[:, c : c + step] = y[96:99]
+    copies = []
+    for part in range(2):
+        half = slice(part * cells // 2, (part + 1) * cells // 2)
+        for c in range(half.start, half.stop, step):
+            b = b_s[:, c : c + step]
+            y = jnp.dot(lhs, b, preferred_element_type=F32)
+            wide = b[0:32].astype(F32) + b[32:64].astype(F32)
+            for d in range(3):
+                spread_ref[d : d + 1, c : c + step] = jnp.sum(
+                    y[32 * d : 32 * d + 32] * wide, axis=0, keepdims=True
+                )
+            mean_ref[:, c : c + step] = y[96:99]
+        for k, (ref, hbm) in enumerate(((mean_ref, mean_hbm), (spread_ref, spread_hbm))):
+            copies.append(pltpu.make_async_copy(ref.at[:, half], hbm.at[:, half], sems.at[part, k]))
+            copies[-1].start()
+    for copy in copies:
+        copy.wait()
 
 
 def shape(*dims, dtype=F32):
@@ -482,8 +476,10 @@
     return tuple(pltpu.with_memory_space_constraint(x, pltpu.VMEM) for x in xs)
 
 
-def call(kernel, out, scratch=(), in_specs=None, name=None):
+def call(kernel, out, scratch=(), in_specs=None, name=None, out_specs=None):
     extra = {} if in_specs is None else {"in_specs": in_specs}
+    if out_specs is not None:
+        extra["out_specs"] = out_specs
     return pl.pallas_call(
         kernel, out_shape=out, scratch_shapes=list(scratch), compiler_params=PARAMS, name=name, **extra
     )
@@ -491,6 +487,7 @@
 
 VM = pl.BlockSpec(memory_space=pltpu.VMEM)
 SM = pl.BlockSpec(memory_space=pltpu.SMEM)
+ANY = pl.BlockSpec(memory_space=pl.ANY)
 
 
 def body(
@@ -511,14 +508,22 @@
             pltpu.VMEM((3, 128, 2048), BF16),
             pltpu.SemaphoreType.DMA,
         ],
-        in_specs=[VM, VM, VM, VM, pl.BlockSpec(memory_space=pl.ANY)],
+        in_specs=[VM, VM, VM, VM, ANY],
         name="buckets",
     )(owner, obs_offset, obs_value, obs_weight, bt)
     recv = lax.all_to_all(send, "space", 0, 0, tiled=True)
-    ft, fp = call(
-        field_kernel, (pltpu.VMEM((32, cells), F32), pltpu.VMEM((96, cells), BF16)), name="field"
-    )(bt, probe_t, scale)
-    recv, ft, fp = on_chip(recv, ft, fp)
+    ft, fp, scaled_probe, days = call(
+        field_kernel,
+        (
+            pltpu.VMEM((32, cells), F32),
+            pltpu.VMEM((96, cells), BF16),
+            pltpu.VMEM((40, 64), F32),
+            pltpu.VMEM((24, 128), F32),
+        ),
+        in_specs=[VM, VM, VM, VM, VM, SM],
+        name="field",
+    )(bt, probe_t, scale, decay, decay.T, inflation)
+    recv, ft, fp, scaled_probe, days = on_chip(recv, ft, fp, scaled_probe, days)
     payload = call(
         gram_kernel,
         pltpu.VMEM((32, 16, 128), F32),
@@ -533,25 +538,26 @@
     )(recv, ft, fp)
     recv_2 = lax.all_to_all(payload, "space", 0, 0, tiled=True)
     (recv_2,) = on_chip(recv_2)
-    both = call(total_kernel, pltpu.VMEM((8, 24, 128), F32), in_specs=[VM, VM, VM, SM], name="totals")(
-        recv_2, decay, decay.T, inflation
-    )
+    both = call(total_kernel, pltpu.VMEM((8, 24, 128), F32), name="totals")(recv_2, days)
     recv_3 = lax.all_to_all(both, "tm", 0, 0, tiled=True)
     (recv_3,) = on_chip(recv_3)
-    basis = call(
-        setup_kernel,
-        pltpu.VMEM((96, cells + 128), BF16),
-        name="setup",
-    )(recv_2, probe_t, scale, fp)
-    (basis,) = on_chip(basis)
-    pos = lax.axis_index("tm").astype(I32).reshape(1)
+    small = call(setup_kernel, pltpu.VMEM((32, 128), F32), name="setup")(recv_2, scaled_probe)
+    (small,) = on_chip(small)
     mean, spread = call(
         solve_kernel,
         (shape(3, cells), shape(3, cells)),
-        [pltpu.VMEM((25, 32, 128), F32), pltpu.VMEM((32, 1024), F32)],
-        in_specs=[SM, VM, VM],
+        [
+            pltpu.VMEM((25, 32, 128), F32),
+            pltpu.VMEM((32, 1024), F32),
+            pltpu.VMEM((96, cells), BF16),
+            pltpu.VMEM((3, cells), F32),
+            pltpu.VMEM((3, cells), F32),
+            pltpu.SemaphoreType.DMA((2, 2)),
+        ],
+        in_specs=[VM, VM, VM],
+        out_specs=(ANY, ANY),
         name="solve",
-    )(pos, recv_3, basis)
+    )(recv_3, small, fp)
     return mean, spread
 
 

time: 77.8 us -> 76.1 us (0.978)
  blocking collectives: 0 us -> 14.3 us
  waiting for transfers between devices: 18.5 us -> 8.91 us
  starting transfers between devices: 24.2 us -> 20.1 us
  Pallas kernels: 33.1 us -> 30.8 us
    all_to_all x0 -> x1, blocking collectives: none -> 14.3 us  [body(): recv_2 = lax.all_to_all(payload, 'space', 0, 0, tiled=True)]
    all_to_all x1 -> x0, waiting for transfers between devices: 9.7 us -> none  [body(): recv_2 = lax.all_to_all(payload, 'space', 0, 0, tiled=True)]
    all_to_all x1 -> x0, starting transfers between devices: 4.13 us -> none  [body(): recv_2 = lax.all_to_all(payload, 'space', 0, 0, tiled=True)]
    pallas_call x2, Pallas kernels: 5.71 us -> 4.04 us  [the longest x1 3.36 us: body(): call(setup_kernel, pltpu.VMEM((32, 128), F32), name='setup')]
    all_to_all x1, waiting for transfers between devices: 0.8 us -> 1.62 us  [body(): recv_3 = lax.all_to_all(both, 'tm', 0, 0, tiled=True)]
  transfers between devices with their start and end apart: 3 -> 2, of which waited for: 3 -> 2; matrix products, arithmetic and copies ran while one was open for 1% -> 1% of each run, Pallas kernels for 7% -> 7%
where the time goes in v4:
time: 76.1 us; the launch traced here: 75.7 us
  Pallas kernels  30.8 us (40%)
  starting transfers between devices  20.1 us (26%)
  blocking collectives  14.3 us (19%)
  waiting for transfers between devices  8.91 us (12%)
  between operations  0.84 us (1%)
    pallas_call x1, Pallas kernels, body(): call(solve_kernel, (shape(3, cells), shape(3, cells)), [pltpu.VMEM((25, 3...  16 us
    all_to_all x1, blocking collectives, body(): recv_2 = lax.all_to_all(payload, 'space', 0, 0, tiled=True)  14.3 us
    all_to_all x1, starting transfers between devices, body(): recv = lax.all_to_all(send, 'space', 0, 0, tiled=True)  11.9 us
    all_to_all x1, starting transfers between devices, body(): recv_3 = lax.all_to_all(both, 'tm', 0, 0, tiled=True)  8.22 us
    all_to_all x1, waiting for transfers between devices, body(): recv = lax.all_to_all(send, 'space', 0, 0, tiled=True)  7.29 us
    pallas_call x1, Pallas kernels, body(): call(gram_kernel, pltpu.VMEM((32, 16, 128), F32), [pltpu.VMEM((3, 256, 40...  5.11 us
    pallas_call x1, Pallas kernels, body(): call(bucket_kernel, pltpu.VMEM((32, 1, 1280), F32), [pltpu.VMEM(bt.shape,...  4.03 us
    pallas_call x1, Pallas kernels, body(): call(setup_kernel, pltpu.VMEM((32, 128), F32), name='setup')  3.36 us
  transfers between devices with their start and end apart: 2, of which 2 were waited for; matrix products, arithmetic and copies ran while one was open for 1% of the time, Pallas kernels for 7%

profile of v4, /device:TPU:1, one launch (start us, length us, event | category | flops | bytes accessed | tf_op | source)
XLA Modules:
  0.0 75.7 jit_solution(14896761037059548385)
XLA Ops:
  0.6 0.0 copy-start
  0.6 4.0 %buckets.1 = f32[32,1,1280]{2,1,0:T(1,128)} custom-call(s32[3,1,2048]{2,1,0:T(1,128)} %bitcast.8, s32[3,2048]{1,0:T(4,128)} %off_ref.1, f32[3,2048]{1,0:T(4,128)} %val_ref.1, f32[3,2048]{1,0:T(4,128)} %wgt_ref.1, bf16[64,8192]{1,0:T(8,128)(2,1)} %bitcast.5), custom_call_target="tpu_custom_call" | custom-call | tf_op jit(solution)/shard_map/buckets/pallas_call | solution.py:501
  4.7 11.9 %all-to-all-start = ((f32[32,1,1280]{2,1,0:T(1,128)}), f32[32,1,1280]{2,1,0:T(1,128)S(1)}, u32[]{:S(2)}, u32[]{:S(2)}) async-start(f32[32,1,1280]{2,1,0:T(1,128)} %buckets.1), calls=%async_computation | async-start | bytes 327680 | tf_op jit(solution)/shard_map/all_to_all | solution.py:514
  16.6 0.0 copy-done
  16.6 0.7 copy.11
  17.3 1.6 %field.1 = (f32[32,8192]{1,0:T(8,128)S(1)}, bf16[96,8192]{1,0:T(8,128)(2,1)S(1)}, f32[40,64]{1,0:T(8,128)S(1)}, f32[24,128]{1,0:T(8,128)S(1)}) custom-call(bf16[64,8192]{1,0:T(8,128)(2,1)} %bitcast.6, bf16[32,64]{1,0:T(8,128)(2,1)} %bitcast.9, f32[1,64]{1,0:T(1,128)} %bitcast.10, f32[3,32]{1,0:T(4,128)} %decay_ref.1, f32[32,3]{1,0:T(8,128)} %bitcast.7, ...), custom_call_target="tpu_custom_call" | custom-call | tf_op jit(solution)/shard_map/field/pallas_call | solution.py:515
  18.9 7.3 %all-to-all-done.recv_ref = f32[32,1,1280]{2,1,0:T(1,128)S(1)} async-done(((f32[32,1,1280]{2,1,0:T(1,128)}), f32[32,1,1280]{2,1,0:T(1,128)S(1)}, u32[]{:S(2)}, u32[]{:S(2)}) %all-to-all-start) | async-done | bytes 163872 | tf_op jit(solution)/shard_map/all_to_all | solution.py:514
  26.2 5.1 %grams.1 = f32[32,16,128]{2,1,0:T(8,128)S(1)} custom-call(f32[32,1,1280]{2,1,0:T(1,128)S(1)} %all-to-all-done.recv_ref, f32[32,8192]{1,0:T(8,128)S(1)} %get-tuple-element.6.ft_ref, bf16[96,8192]{1,0:T(8,128)(2,1)S(1)} %get-tuple-element.7.fp_ref), custom_call_target="tpu_custom_call" | custom-call | tf_op jit(solution)/shard_map/grams/pallas_call | solution.py:527
  31.3 14.3 %all_to_all.15.recv_ref = f32[32,16,128]{2,1,0:T(8,128)S(1)} all-to-all(f32[32,16,128]{2,1,0:T(8,128)S(1)} %grams.1), channel_id=1, replica_groups=mesh['tm'=8,'space'=32] {'space'}, dimensions={0} | all-to-all | bytes 524288 | tf_op jit(solution)/shard_map/all_to_all | solution.py:539
  45.6 0.7 totals.1
  46.3 8.2 %all-to-all-start.2 = ((f32[8,24,128]{2,1,0:T(8,128)}), f32[8,24,128]{2,1,0:T(8,128)S(1)}, u32[]{:S(2)}, u32[]{:S(2)}) async-start(f32[8,24,128]{2,1,0:T(8,128)} %totals.1), calls=%async_computation.2 | async-start | bytes 196608 | tf_op jit(solution)/shard_map/all_to_all | solution.py:542
  54.5 3.4 %setup.1.small_ref = f32[32,128]{1,0:T(8,128)S(1)} custom-call(f32[32,16,128]{2,1,0:T(8,128)S(1)} %all_to_all.15.recv_ref, f32[40,64]{1,0:T(8,128)S(1)} %get-tuple-element.9.probe_ref), custom_call_target="tpu_custom_call" | custom-call | tf_op jit(solution)/shard_map/setup/pallas_call | solution.py:544
  57.9 1.6 %all-to-all-done.2.recv_ref = f32[8,24,128]{2,1,0:T(8,128)S(1)} async-done(((f32[8,24,128]{2,1,0:T(8,128)}), f32[8,24,128]{2,1,0:T(8,128)S(1)}, u32[]{:S(2)}, u32[]{:S(2)}) %all-to-all-start.2) | async-done | bytes 98336 | tf_op jit(solution)/shard_map/all_to_all | solution.py:542
  59.5 16.0 %solve.1 = (f32[3,8192]{1,0:T(4,128)}, f32[3,8192]{1,0:T(4,128)}) custom-call(f32[8,24,128]{2,1,0:T(8,128)S(1)} %all-to-all-done.2.recv_ref, f32[32,128]{1,0:T(8,128)S(1)} %setup.1.small_ref, bf16[96,8192]{1,0:T(8,128)(2,1)S(1)} %get-tuple-element.7.fp_ref), custom_call_target="tpu_custom_call" | custom-call | tf_op jit(solution)/shard_map/solve/pallas_call | solution.py:546
Async XLA Ops:
  0.6 15.9 %copy-start = (f32[3,32]{1,0:T(4,128)S(1)}, f32[3,32]{1,0:T(4,128)}, u32[]{:S(2)}) copy-start(f32[3,32]{1,0:T(4,128)} %decay_ref.1) | copy-start | bytes 1156
  4.7 21.5 %all-to-all-start = ((f32[32,1,1280]{2,1,0:T(1,128)}), f32[32,1,1280]{2,1,0:T(1,128)S(1)}, u32[]{:S(2)}, u32[]{:S(2)}) async-start(f32[32,1,1280]{2,1,0:T(1,128)} %buckets.1), calls=%async_computation | async-start | bytes 327680 | tf_op jit(solution)/shard_map/all_to_all | solution.py:514
  46.3 13.2 %all-to-all-start.2 = ((f32[8,24,128]{2,1,0:T(8,128)}), f32[8,24,128]{2,1,0:T(8,128)S(1)}, u32[]{:S(2)}, u32[]{:S(2)}) async-start(f32[8,24,128]{2,1,0:T(8,128)} %totals.1), calls=%async_computation.2 | async-start | bytes 196608 | tf_op jit(solution)/shard_map/all_to_all | solution.py:542

commit v5 on v4

--- a/solution.py
+++ b/solution.py
@@ -48,7 +48,7 @@
     return iota((rows, LANES), 0).astype(F32).astype(BF16)
 
 
-def bucket_kernel(owner_ref, off_ref, val_ref, wgt_ref, bt_hbm, send_ref, bt_ref, oh_s, lhs_s, rt_s, sem):
+def bucket_kernel(owner_ref, off_ref, val_ref, wgt_ref, bt_hbm, send_ref, bt_ref, oh_s, sem):
     fetch = pltpu.make_async_copy(bt_hbm, bt_ref, sem)
     fetch.start()
     days, _, obs = owner_ref.shape
@@ -68,27 +68,31 @@
     counts = jnp.dot(oh_s[...], counter, preferred_element_type=F32)
     for d in range(days):
         base = jnp.zeros((owners, LANES), F32)
-        for c in range(chunks):
-            at = slice(c * LANES, (c + 1) * LANES)
-            k = (d * chunks + c) * owners
-            one_hot = oh_s[k : k + owners]
-            count = counts[k : k + owners]
-            slot = jnp.sum(
-                one_hot.astype(F32) * (count[:, :LANES] + base), axis=0, keepdims=True
-            )
-            base = base + count[:, LANES:]
-            rt_s[d, :, at] = jnp.where(sub_slot == packed(slot, LANES), one, zero)
-            weight = wgt_ref[d : d + 1, at]
-            offset = off_ref[d : d + 1, at]
-            fields = (
-                *halves(weight),
-                *halves(weight * val_ref[d : d + 1, at]),
-                (offset >> 7).astype(F32),
-                (offset & 127).astype(F32),
-            )
-            for f, row in enumerate(fields):
-                lhs_s[d, f * owners : (f + 1) * owners, at] = one_hot * packed(row, owners)
-        got = nt(lhs_s[d], rt_s[d])
+        got = jnp.zeros((6 * owners, LANES), F32)
+        for begin in range(0, chunks, 4):
+            lefts, rights = [], []
+            for c in range(begin, begin + 4):
+                at = slice(c * LANES, (c + 1) * LANES)
+                k = (d * chunks + c) * owners
+                one_hot = oh_s[k : k + owners]
+                count = counts[k : k + owners]
+                slot = jnp.sum(
+                    one_hot.astype(F32) * (count[:, :LANES] + base), axis=0, keepdims=True
+                )
+                base = base + count[:, LANES:]
+                rights.append(jnp.where(sub_slot == packed(slot, LANES), one, zero))
+                weight = wgt_ref[d : d + 1, at]
+                offset = off_ref[d : d + 1, at]
+                fields = (
+                    *halves(weight),
+                    *halves(weight * val_ref[d : d + 1, at]),
+                    (offset >> 7).astype(F32),
+                    (offset & 127).astype(F32),
+                )
+                lefts.append(
+                    jnp.concatenate([one_hot * packed(row, owners) for row in fields], axis=0)
+                )
+            got = got + nt(jnp.concatenate(lefts, axis=1), jnp.concatenate(rights, axis=1))
         part = [got[f * owners : (f + 1) * owners] for f in range(6)]
         for f, x in enumerate((part[0] + part[1], part[2] + part[3], part[4] * 128.0 + part[5])):
             j = f * days + d
@@ -115,8 +119,8 @@
     columns = jnp.zeros((16, LANES), F32)
     first, second = [], []
     for d in range(3):
-        columns = jnp.where(lane16 == 105 + 2 * d, decay_t_ref[:16, d : d + 1], columns)
-        columns = jnp.where(lane16 == 106 + 2 * d, decay_t_ref[16:, d : d + 1], columns)
+        columns = jnp.where(lane16 == 105 + d, decay_t_ref[:16, d : d + 1], columns)
+        columns = jnp.where(lane16 == 108 + d, decay_t_ref[16:, d : d + 1], columns)
         gamma = 1.0 / infl_ref[d]
         decay = jnp.concatenate([decay_ref[d : d + 1, :]] * 4, axis=1)
         right = (lane1 >= 64) & (lane1 < 96)
@@ -126,7 +130,7 @@
     days_ref[...] = jnp.concatenate([columns] + rows, axis=0)
 
 
-def gram_kernel(recv_ref, ft_ref, fp_ref, out_ref, lhs_s, rhs_s, wc_s, uc_s, pay_s):
+def gram_kernel(recv_ref, ft_ref, fp_ref, out_ref, wc_s, uc_s, pay_s):
     readers = recv_ref.shape[0]
     days = 3
     sub64, sub128 = counter16(64), counter16(LANES)
@@ -137,13 +141,18 @@
         u = halves(recv_ref[:, 0, (3 + d) * LANES : (4 + d) * LANES])
         offset = recv_ref[:, 0, (6 + d) * LANES : (7 + d) * LANES].astype(I32)
         high, low = (offset >> 7).astype(F32), (offset & 127).astype(F32)
-        for r in range(readers):
-            at = slice(r * LANES, (r + 1) * LANES)
-            hit = sub64 == packed(high[r : r + 1], 64)
-            for f, x in enumerate(w + u):
-                lhs_s[d, f * 64 : (f + 1) * 64, at] = jnp.where(hit, packed(x[r : r + 1], 64), zero)
-            rhs_s[d, :, at] = jnp.where(sub128 == packed(low[r : r + 1], LANES), one, zero)
-        got = nt(lhs_s[d], rhs_s[d])
+        got = jnp.zeros((256, LANES), F32)
+        for begin in range(0, readers, 4):
+            lefts, rights = [], []
+            for r in range(begin, begin + 4):
+                hit = sub64 == packed(high[r : r + 1], 64)
+                lefts.append(
+                    jnp.concatenate(
+                        [jnp.where(hit, packed(x[r : r + 1], 64), zero) for x in w + u], axis=0
+                    )
+                )
+                rights.append(jnp.where(sub128 == packed(low[r : r + 1], LANES), one, zero))
+            got = got + nt(jnp.concatenate(lefts, axis=1), jnp.concatenate(rights, axis=1))
         wc_s[d] = got[:64] + got[64:128]
         uc_s[d] = got[128:192] + got[192:]
     accs = [jnp.zeros((RANK, LANES), F32)] * days
@@ -176,8 +185,8 @@
         pieces += [jnp.where(r16 <= c16, sym[:16, :16], low), sym[:16, 16:]]
         diag = jnp.sum(jnp.where(r16 == c16, low, 0.0), axis=1, keepdims=True)
         g = jnp.sum(accs[d], axis=1, keepdims=True)
-        pay = jnp.where(lane16 == 96 + 2 * d, g[:16], pay)
-        pay = jnp.where(lane16 == 97 + 2 * d, g[16:], pay)
+        pay = jnp.where(lane16 == 96 + d, g[:16], pay)
+        pay = jnp.where(lane16 == 99 + d, g[16:], pay)
         pay = jnp.where(lane16 == 102 + d, diag, pay)
     pay_s[...] = pay
     for k, piece in enumerate(pieces):
@@ -298,6 +307,23 @@
     small_ref[...] = jnp.concatenate([linv, prec, zero64], axis=1)
 
 
+def unfold(x, roll):
+    row, lane = iota((16, LANES), 0), iota((16, LANES), 1)
+    col = lane & 15
+    turned = jnp.transpose(x)
+    turned = jnp.concatenate([turned[16 * b : 16 * b + 16] for b in range(8)], axis=1)
+    top = jnp.where((lane < 96) & ((lane & 16) == 0) & (row > col), turned, x)
+    diag = jnp.zeros((16, LANES), F32)
+    for d in range(3):
+        diag = jnp.where((lane >> 5) == d, x[:, 102 + d : 103 + d], diag)
+    corner = roll(jnp.where(row > col, x, turned), 16, 1)
+    corner = jnp.where(row == col, diag, corner)
+    low = jnp.where((lane & 16) == 0, roll(turned, LANES - 16, 1), corner)
+    low = jnp.where(lane < 96, low, roll(x, LANES - 3, 1))
+    both = jnp.concatenate([top, low], axis=0)
+    return jnp.where(iota((32, LANES), 1) < 99, both, 0.0)
+
+
 def solve_kernel(recv_ref, small_ref, fp_ref, mean_hbm, spread_hbm, e_s, x_s, b_s, mean_ref, spread_ref, sems):
     lane = iota((32, LANES), 1)
     linv, prec = small_ref[:, :32], small_ref[:, 32:64]
@@ -322,37 +348,14 @@
         ],
         axis=0,
     )
-    r16, c16 = iota((16, 16), 0), iota((16, 16), 1)
     zero_row = jnp.zeros((1, LANES), F32)
     dcols = []
     for r in range(8):
         x = recv_ref[r, :16, :]
-        xt = jnp.transpose(x)
-        slabs = []
+        x_s[:, r * LANES : (r + 1) * LANES] = unfold(x, pltpu.roll)
         for d in range(3):
-            a = x[:, 32 * d : 32 * d + 16]
-            q = x[:, 32 * d + 16 : 32 * d + 32]
-            at = xt[32 * d : 32 * d + 16]
-            qt = xt[32 * d + 16 : 32 * d + 32]
-            p = jnp.where(r16 <= c16, a, at)
-            low = jnp.where(r16 == c16, x[:, 102 + d : 103 + d], jnp.where(r16 > c16, a, at))
-            slabs.append(
-                jnp.concatenate(
-                    [jnp.concatenate([p, q], axis=1), jnp.concatenate([qt, low], axis=1)], axis=0
-                )
-            )
-            dcols.append(
-                jnp.concatenate(
-                    [x[:, 105 + 2 * d : 106 + 2 * d], x[:, 106 + 2 * d : 107 + 2 * d]], axis=0
-                )
-            )
-        gs = [
-            jnp.concatenate([x[:, 96 + 2 * d : 97 + 2 * d], x[:, 97 + 2 * d : 98 + 2 * d]], axis=0)
-            for d in range(3)
-        ]
-        x_s[:, r * LANES : (r + 1) * LANES] = jnp.concatenate(
-            slabs + gs + [jnp.zeros((32, 29), F32)], axis=1
-        )
+            column = (x[:, 105 + d : 106 + d], x[:, 108 + d : 109 + d])
+            dcols.append(jnp.concatenate(column, axis=0))
     z = nn_high(linv, x_s[...])
     zs = jnp.concatenate([z[:, r * LANES : (r + 1) * LANES] for r in range(8)], axis=0)
     hs = nn_high(zs, per_day)
@@ -504,8 +507,6 @@
         [
             pltpu.VMEM(bt.shape, BF16),
             pltpu.VMEM((3 * 16 * 32, 128), BF16),
-            pltpu.VMEM((3, 192, 2048), BF16),
-            pltpu.VMEM((3, 128, 2048), BF16),
             pltpu.SemaphoreType.DMA,
         ],
         in_specs=[VM, VM, VM, VM, ANY],
@@ -528,8 +529,6 @@
         gram_kernel,
         pltpu.VMEM((32, 16, 128), F32),
         [
-            pltpu.VMEM((3, 256, 4096), BF16),
-            pltpu.VMEM((3, 128, 4096), BF16),
             pltpu.VMEM((3, 64, 128), F32),
             pltpu.VMEM((3, 64, 128), F32),
             pltpu.VMEM((16, 128), F32),

time: 76.1 us -> 73.6 us (0.967)
  Pallas kernels: 30.8 us -> 28.3 us
    pallas_call x1, Pallas kernels: 16 us -> 14.6 us  [body(): call(solve_kernel, (shape(3, cells), shape(3, cells)), [pltpu.VMEM((25, 3...]
where the time goes in v5:
time: 73.6 us; the launch traced here: 73.2 us
  Pallas kernels  28.3 us (38%)
  starting transfers between devices  20.1 us (27%)
  blocking collectives  14.3 us (19%)
  waiting for transfers between devices  8.91 us (12%)
  between operations  0.84 us (1%)
    pallas_call x1, Pallas kernels, body(): call(solve_kernel, (shape(3, cells), shape(3, cells)), [pltpu.VMEM((25, 3...  14.6 us
    all_to_all x1, blocking collectives, body(): recv_2 = lax.all_to_all(payload, 'space', 0, 0, tiled=True)  14.3 us
    all_to_all x1, starting transfers between devices, body(): recv = lax.all_to_all(send, 'space', 0, 0, tiled=True)  11.9 us
    all_to_all x1, starting transfers between devices, body(): recv_3 = lax.all_to_all(both, 'tm', 0, 0, tiled=True)  8.22 us
    all_to_all x1, waiting for transfers between devices, body(): recv = lax.all_to_all(send, 'space', 0, 0, tiled=True)  7.29 us
    pallas_call x1, Pallas kernels, body(): call(gram_kernel, pltpu.VMEM((32, 16, 128), F32), [pltpu.VMEM((3, 64, 128...  4.52 us
    pallas_call x1, Pallas kernels, body(): call(bucket_kernel, pltpu.VMEM((32, 1, 1280), F32), [pltpu.VMEM(bt.shape,...  3.53 us
    pallas_call x1, Pallas kernels, body(): call(setup_kernel, pltpu.VMEM((32, 128), F32), name='setup')  3.36 us
  transfers between devices with their start and end apart: 2, of which 2 were waited for; matrix products, arithmetic and copies ran while one was open for 1% of the time, Pallas kernels for 7%

profile of v5, /device:TPU:1, one launch (start us, length us, event | category | flops | bytes accessed | tf_op | source)
XLA Modules:
  0.0 73.2 jit_solution(9495208435711018051)
XLA Ops:
  0.6 0.0 copy-start
  0.6 3.5 %buckets.1 = f32[32,1,1280]{2,1,0:T(1,128)} custom-call(s32[3,1,2048]{2,1,0:T(1,128)} %bitcast.8, s32[3,2048]{1,0:T(4,128)} %off_ref.1, f32[3,2048]{1,0:T(4,128)} %val_ref.1, f32[3,2048]{1,0:T(4,128)} %wgt_ref.1, bf16[64,8192]{1,0:T(8,128)(2,1)} %bitcast.5), custom_call_target="tpu_custom_call" | custom-call | tf_op jit(solution)/shard_map/buckets/pallas_call | solution.py:504
  4.2 11.9 %all-to-all-start = ((f32[32,1,1280]{2,1,0:T(1,128)}), f32[32,1,1280]{2,1,0:T(1,128)S(1)}, u32[]{:S(2)}, u32[]{:S(2)}) async-start(f32[32,1,1280]{2,1,0:T(1,128)} %buckets.1), calls=%async_computation | async-start | bytes 327680 | tf_op jit(solution)/shard_map/all_to_all | solution.py:515
  16.1 0.0 copy-done
  16.1 0.7 copy.11
  16.8 1.6 %field.1 = (f32[32,8192]{1,0:T(8,128)S(1)}, bf16[96,8192]{1,0:T(8,128)(2,1)S(1)}, f32[40,64]{1,0:T(8,128)S(1)}, f32[24,128]{1,0:T(8,128)S(1)}) custom-call(bf16[64,8192]{1,0:T(8,128)(2,1)} %bitcast.6, bf16[32,64]{1,0:T(8,128)(2,1)} %bitcast.9, f32[1,64]{1,0:T(1,128)} %bitcast.10, f32[3,32]{1,0:T(4,128)} %decay_ref.1, f32[32,3]{1,0:T(8,128)} %bitcast.7, ...), custom_call_target="tpu_custom_call" | custom-call | tf_op jit(solution)/shard_map/field/pallas_call | solution.py:516
  18.4 7.3 %all-to-all-done.recv_ref = f32[32,1,1280]{2,1,0:T(1,128)S(1)} async-done(((f32[32,1,1280]{2,1,0:T(1,128)}), f32[32,1,1280]{2,1,0:T(1,128)S(1)}, u32[]{:S(2)}, u32[]{:S(2)}) %all-to-all-start) | async-done | bytes 163872 | tf_op jit(solution)/shard_map/all_to_all | solution.py:515
  25.7 4.5 %grams.1 = f32[32,16,128]{2,1,0:T(8,128)S(1)} custom-call(f32[32,1,1280]{2,1,0:T(1,128)S(1)} %all-to-all-done.recv_ref, f32[32,8192]{1,0:T(8,128)S(1)} %get-tuple-element.6.ft_ref, bf16[96,8192]{1,0:T(8,128)(2,1)S(1)} %get-tuple-element.7.fp_ref), custom_call_target="tpu_custom_call" | custom-call | tf_op jit(solution)/shard_map/grams/pallas_call | solution.py:528
  30.2 14.3 %all_to_all.15.recv_ref = f32[32,16,128]{2,1,0:T(8,128)S(1)} all-to-all(f32[32,16,128]{2,1,0:T(8,128)S(1)} %grams.1), channel_id=1, replica_groups=mesh['tm'=8,'space'=32] {'space'}, dimensions={0} | all-to-all | bytes 524288 | tf_op jit(solution)/shard_map/all_to_all | solution.py:538
  44.5 0.7 totals.1
  45.2 8.2 %all-to-all-start.2 = ((f32[8,24,128]{2,1,0:T(8,128)}), f32[8,24,128]{2,1,0:T(8,128)S(1)}, u32[]{:S(2)}, u32[]{:S(2)}) async-start(f32[8,24,128]{2,1,0:T(8,128)} %totals.1), calls=%async_computation.2 | async-start | bytes 196608 | tf_op jit(solution)/shard_map/all_to_all | solution.py:541
  53.4 3.4 %setup.1.small_ref = f32[32,128]{1,0:T(8,128)S(1)} custom-call(f32[32,16,128]{2,1,0:T(8,128)S(1)} %all_to_all.15.recv_ref, f32[40,64]{1,0:T(8,128)S(1)} %get-tuple-element.9.probe_ref), custom_call_target="tpu_custom_call" | custom-call | tf_op jit(solution)/shard_map/setup/pallas_call | solution.py:543
  56.8 1.6 %all-to-all-done.2.recv_ref = f32[8,24,128]{2,1,0:T(8,128)S(1)} async-done(((f32[8,24,128]{2,1,0:T(8,128)}), f32[8,24,128]{2,1,0:T(8,128)S(1)}, u32[]{:S(2)}, u32[]{:S(2)}) %all-to-all-start.2) | async-done | bytes 98336 | tf_op jit(solution)/shard_map/all_to_all | solution.py:541
  58.4 14.6 %solve.1 = (f32[3,8192]{1,0:T(4,128)}, f32[3,8192]{1,0:T(4,128)}) custom-call(f32[8,24,128]{2,1,0:T(8,128)S(1)} %all-to-all-done.2.recv_ref, f32[32,128]{1,0:T(8,128)S(1)} %setup.1.small_ref, bf16[96,8192]{1,0:T(8,128)(2,1)S(1)} %get-tuple-element.7.fp_ref), custom_call_target="tpu_custom_call" | custom-call | tf_op jit(solution)/shard_map/solve/pallas_call | solution.py:545
Async XLA Ops:
  0.6 15.4 %copy-start = (f32[3,32]{1,0:T(4,128)S(1)}, f32[3,32]{1,0:T(4,128)}, u32[]{:S(2)}) copy-start(f32[3,32]{1,0:T(4,128)} %decay_ref.1) | copy-start | bytes 1156
  4.2 21.5 %all-to-all-start = ((f32[32,1,1280]{2,1,0:T(1,128)}), f32[32,1,1280]{2,1,0:T(1,128)S(1)}, u32[]{:S(2)}, u32[]{:S(2)}) async-start(f32[32,1,1280]{2,1,0:T(1,128)} %buckets.1), calls=%async_computation | async-start | bytes 327680 | tf_op jit(solution)/shard_map/all_to_all | solution.py:515
  45.2 13.2 %all-to-all-start.2 = ((f32[8,24,128]{2,1,0:T(8,128)}), f32[8,24,128]{2,1,0:T(8,128)S(1)}, u32[]{:S(2)}, u32[]{:S(2)}) async-start(f32[8,24,128]{2,1,0:T(8,128)} %totals.1), calls=%async_computation.2 | async-start | bytes 196608 | tf_op jit(solution)/shard_map/all_to_all | solution.py:541

commit v6 on v5

--- a/solution.py
+++ b/solution.py
@@ -136,7 +136,7 @@
     sub64, sub128 = counter16(64), counter16(LANES)
     one, zero = jnp.ones((), BF16), jnp.zeros((), BF16)
 
-    for d in range(days):
+    def counting(d):
         w = halves(recv_ref[:, 0, d * LANES : (d + 1) * LANES])
         u = halves(recv_ref[:, 0, (3 + d) * LANES : (4 + d) * LANES])
         offset = recv_ref[:, 0, (6 + d) * LANES : (7 + d) * LANES].astype(I32)
@@ -153,23 +153,32 @@
                 )
                 rights.append(jnp.where(sub128 == packed(low[r : r + 1], LANES), one, zero))
             got = got + nt(jnp.concatenate(lefts, axis=1), jnp.concatenate(rights, axis=1))
+            yield
         wc_s[d] = got[:64] + got[64:128]
         uc_s[d] = got[128:192] + got[192:]
-    accs = [jnp.zeros((RANK, LANES), F32)] * days
-    prod = jnp.zeros((days * 64, 64), F32)
-    for start in range(0, 64, 4):
-        xs = []
-        for h in range(start, start + 4):
-            ft = ft_ref[:, h * LANES : (h + 1) * LANES]
-            pieces = []
-            for d in range(days):
+
+    accs, prods = [None] * days, [None] * days
+
+    def weighing(d):
+        acc, prod = jnp.zeros((RANK, LANES), F32), jnp.zeros((64, 64), F32)
+        for start in range(0, 64, 4):
+            xs = []
+            for h in range(start, start + 4):
+                ft = ft_ref[:, h * LANES : (h + 1) * LANES]
                 x = ft * wc_s[d, h : h + 1, :]
                 top = x.astype(BF16)
-                pieces += [top, (x - top.astype(F32)).astype(BF16)]
-                accs[d] = accs[d] + ft * uc_s[d, h : h + 1, :]
-            xs.append(jnp.concatenate(pieces, axis=0))
-        x = jnp.concatenate(xs, axis=1)
-        prod = prod + nt(x, fp_ref[0:64, start * LANES : (start + 4) * LANES])
+                xs.append(jnp.concatenate([top, (x - top.astype(F32)).astype(BF16)], axis=0))
+                acc = acc + ft * uc_s[d, h : h + 1, :]
+            x = jnp.concatenate(xs, axis=1)
+            prod = prod + nt(x, fp_ref[0:64, start * LANES : (start + 4) * LANES])
+            yield
+        accs[d], prods[d] = acc, prod
+
+    for d in range(days + 1):
+        work = [counting(d)] if d < days else []
+        work += [weighing(d - 1)] if d else []
+        while work:
+            work = [w for w in work if next(w, "done") != "done"]
     chunk = jnp.sum(recv_ref[:, 0, 9 * LANES : 10 * LANES], axis=0, keepdims=True)
     row16, lane16 = iota((16, LANES), 0), iota((16, LANES), 1)
     fold = jnp.where((lane16 >> 3) == row16, chunk, 0.0)
@@ -179,7 +188,7 @@
     r16, c16 = iota((16, 16), 0), iota((16, 16), 1)
     pieces = []
     for d in range(days):
-        p = prod[d * 64 : (d + 1) * 64]
+        p = prods[d]
         sym = p[:32, :32] + p[:32, 32:] + p[32:, :32] + p[32:, 32:]
         low = sym[16:, 16:]
         pieces += [jnp.where(r16 <= c16, sym[:16, :16], low), sym[:16, 16:]]
@@ -329,14 +338,6 @@
     linv, prec = small_ref[:, :32], small_ref[:, 32:64]
     cells = fp_ref.shape[1]
     step = 1024
-    one, two = halves(linv)
-    onto = jnp.concatenate([one, one, two], axis=1).astype(BF16)
-    for c in range(0, cells, step):
-        basis = jnp.dot(onto, fp_ref[:, c : c + step], preferred_element_type=F32)
-        top = basis.astype(BF16)
-        b_s[0:32, c : c + step] = top
-        b_s[32:64, c : c + step] = (basis - top.astype(F32)).astype(BF16)
-        b_s[64:96, c : c + step] = top
     lt = jnp.transpose(linv)
     zero32 = jnp.zeros((32, 32), F32)
     eye = (iota((32, 32), 0) == iota((32, 32), 1)).astype(F32)
@@ -435,6 +436,14 @@
                     i = renew(("r", i, pi), as_right)
                 out.append((j, i))
             rings[target] = out
+    one, two = halves(linv)
+    onto = jnp.concatenate([one, one, two], axis=1).astype(BF16)
+    for c in range(0, cells, step):
+        basis = jnp.dot(onto, fp_ref[:, c : c + step], preferred_element_type=F32)
+        top = basis.astype(BF16)
+        b_s[0:32, c : c + step] = top
+        b_s[32:64, c : c + step] = (basis - top.astype(F32)).astype(BF16)
+        b_s[64:96, c : c + step] = top
     eye_at = jnp.where(lane == iota((32, LANES), 0) + 32, 1.0, 0.0)
     last = []
     for target in range(3):

time: 73.6 us -> 73.3 us (level)
  no operation moved by 1% of the time
where the time goes in v6:
time: 73.3 us; the launch traced here: 72.9 us
  Pallas kernels  28 us (38%)
  starting transfers between devices  20.1 us (27%)
  blocking collectives  14.3 us (20%)
  waiting for transfers between devices  8.91 us (12%)
  between operations  0.84 us (1%)
    pallas_call x1, Pallas kernels, body(): call(solve_kernel, (shape(3, cells), shape(3, cells)), [pltpu.VMEM((25, 3...  14.4 us
    all_to_all x1, blocking collectives, body(): recv_2 = lax.all_to_all(payload, 'space', 0, 0, tiled=True)  14.3 us
    all_to_all x1, starting transfers between devices, body(): recv = lax.all_to_all(send, 'space', 0, 0, tiled=True)  11.9 us
    all_to_all x1, starting transfers between devices, body(): recv_3 = lax.all_to_all(both, 'tm', 0, 0, tiled=True)  8.22 us
    all_to_all x1, waiting for transfers between devices, body(): recv = lax.all_to_all(send, 'space', 0, 0, tiled=True)  7.29 us
    pallas_call x1, Pallas kernels, body(): call(gram_kernel, pltpu.VMEM((32, 16, 128), F32), [pltpu.VMEM((3, 64, 128...  4.39 us
    pallas_call x1, Pallas kernels, body(): call(bucket_kernel, pltpu.VMEM((32, 1, 1280), F32), [pltpu.VMEM(bt.shape,...  3.53 us
    pallas_call x1, Pallas kernels, body(): call(setup_kernel, pltpu.VMEM((32, 128), F32), name='setup')  3.36 us
  transfers between devices with their start and end apart: 2, of which 2 were waited for; matrix products, arithmetic and copies ran while one was open for 1% of the time, Pallas kernels for 7%

profile of v6, /device:TPU:1, one launch (start us, length us, event | category | flops | bytes accessed | tf_op | source)
XLA Modules:
  0.0 72.9 jit_solution(8664073095492931427)
XLA Ops:
  0.6 0.0 copy-start
  0.6 3.5 %buckets.1 = f32[32,1,1280]{2,1,0:T(1,128)} custom-call(s32[3,1,2048]{2,1,0:T(1,128)} %bitcast.8, s32[3,2048]{1,0:T(4,128)} %off_ref.1, f32[3,2048]{1,0:T(4,128)} %val_ref.1, f32[3,2048]{1,0:T(4,128)} %wgt_ref.1, bf16[64,8192]{1,0:T(8,128)(2,1)} %bitcast.5), custom_call_target="tpu_custom_call" | custom-call | tf_op jit(solution)/shard_map/buckets/pallas_call | solution.py:513
  4.2 11.9 %all-to-all-start = ((f32[32,1,1280]{2,1,0:T(1,128)}), f32[32,1,1280]{2,1,0:T(1,128)S(1)}, u32[]{:S(2)}, u32[]{:S(2)}) async-start(f32[32,1,1280]{2,1,0:T(1,128)} %buckets.1), calls=%async_computation | async-start | bytes 327680 | tf_op jit(solution)/shard_map/all_to_all | solution.py:524
  16.1 0.0 copy-done
  16.1 0.7 copy.11
  16.8 1.6 %field.1 = (f32[32,8192]{1,0:T(8,128)S(1)}, bf16[96,8192]{1,0:T(8,128)(2,1)S(1)}, f32[40,64]{1,0:T(8,128)S(1)}, f32[24,128]{1,0:T(8,128)S(1)}) custom-call(bf16[64,8192]{1,0:T(8,128)(2,1)} %bitcast.6, bf16[32,64]{1,0:T(8,128)(2,1)} %bitcast.9, f32[1,64]{1,0:T(1,128)} %bitcast.10, f32[3,32]{1,0:T(4,128)} %decay_ref.1, f32[32,3]{1,0:T(8,128)} %bitcast.7, ...), custom_call_target="tpu_custom_call" | custom-call | tf_op jit(solution)/shard_map/field/pallas_call | solution.py:525
  18.4 7.3 %all-to-all-done.recv_ref = f32[32,1,1280]{2,1,0:T(1,128)S(1)} async-done(((f32[32,1,1280]{2,1,0:T(1,128)}), f32[32,1,1280]{2,1,0:T(1,128)S(1)}, u32[]{:S(2)}, u32[]{:S(2)}) %all-to-all-start) | async-done | bytes 163872 | tf_op jit(solution)/shard_map/all_to_all | solution.py:524
  25.7 4.4 %grams.1 = f32[32,16,128]{2,1,0:T(8,128)S(1)} custom-call(f32[32,1,1280]{2,1,0:T(1,128)S(1)} %all-to-all-done.recv_ref, f32[32,8192]{1,0:T(8,128)S(1)} %get-tuple-element.6.ft_ref, bf16[96,8192]{1,0:T(8,128)(2,1)S(1)} %get-tuple-element.7.fp_ref), custom_call_target="tpu_custom_call" | custom-call | tf_op jit(solution)/shard_map/grams/pallas_call | solution.py:537
  30.1 14.3 %all_to_all.15.recv_ref = f32[32,16,128]{2,1,0:T(8,128)S(1)} all-to-all(f32[32,16,128]{2,1,0:T(8,128)S(1)} %grams.1), channel_id=1, replica_groups=mesh['tm'=8,'space'=32] {'space'}, dimensions={0} | all-to-all | bytes 524288 | tf_op jit(solution)/shard_map/all_to_all | solution.py:547
  44.4 0.7 totals.1
  45.1 8.2 %all-to-all-start.2 = ((f32[8,24,128]{2,1,0:T(8,128)}), f32[8,24,128]{2,1,0:T(8,128)S(1)}, u32[]{:S(2)}, u32[]{:S(2)}) async-start(f32[8,24,128]{2,1,0:T(8,128)} %totals.1), calls=%async_computation.2 | async-start | bytes 196608 | tf_op jit(solution)/shard_map/all_to_all | solution.py:550
  53.3 3.4 %setup.1.small_ref = f32[32,128]{1,0:T(8,128)S(1)} custom-call(f32[32,16,128]{2,1,0:T(8,128)S(1)} %all_to_all.15.recv_ref, f32[40,64]{1,0:T(8,128)S(1)} %get-tuple-element.9.probe_ref), custom_call_target="tpu_custom_call" | custom-call | tf_op jit(solution)/shard_map/setup/pallas_call | solution.py:552
  56.7 1.6 %all-to-all-done.2.recv_ref = f32[8,24,128]{2,1,0:T(8,128)S(1)} async-done(((f32[8,24,128]{2,1,0:T(8,128)}), f32[8,24,128]{2,1,0:T(8,128)S(1)}, u32[]{:S(2)}, u32[]{:S(2)}) %all-to-all-start.2) | async-done | bytes 98336 | tf_op jit(solution)/shard_map/all_to_all | solution.py:550
  58.3 14.4 %solve.1 = (f32[3,8192]{1,0:T(4,128)}, f32[3,8192]{1,0:T(4,128)}) custom-call(f32[8,24,128]{2,1,0:T(8,128)S(1)} %all-to-all-done.2.recv_ref, f32[32,128]{1,0:T(8,128)S(1)} %setup.1.small_ref, bf16[96,8192]{1,0:T(8,128)(2,1)S(1)} %get-tuple-element.7.fp_ref), custom_call_target="tpu_custom_call" | custom-call | tf_op jit(solution)/shard_map/solve/pallas_call | solution.py:554
Async XLA Ops:
  0.6 15.4 %copy-start = (f32[3,32]{1,0:T(4,128)S(1)}, f32[3,32]{1,0:T(4,128)}, u32[]{:S(2)}) copy-start(f32[3,32]{1,0:T(4,128)} %decay_ref.1) | copy-start | bytes 1156
  4.2 21.5 %all-to-all-start = ((f32[32,1,1280]{2,1,0:T(1,128)}), f32[32,1,1280]{2,1,0:T(1,128)S(1)}, u32[]{:S(2)}, u32[]{:S(2)}) async-start(f32[32,1,1280]{2,1,0:T(1,128)} %buckets.1), calls=%async_computation | async-start | bytes 327680 | tf_op jit(solution)/shard_map/all_to_all | solution.py:524
  45.1 13.2 %all-to-all-start.2 = ((f32[8,24,128]{2,1,0:T(8,128)}), f32[8,24,128]{2,1,0:T(8,128)S(1)}, u32[]{:S(2)}, u32[]{:S(2)}) async-start(f32[8,24,128]{2,1,0:T(8,128)} %totals.1), calls=%async_computation.2 | async-start | bytes 196608 | tf_op jit(solution)/shard_map/all_to_all | solution.py:550
